TPU v7x, 32 devices: a whole 2x2x4 slice. The times are simulated.
32 devices in a mesh: dp: 16 (over z, y, x), tensor: 2 (over core).
Axes of the slice: x: 2, y: 2, z: 4, core: 2. Of those that a mesh axis runs over, the one named last changes fastest.
Arguments:
- tokens: bfloat16 [16, 1024, 768], P('dp'), may hold values from -6 to 6
- cotangent: bfloat16 [16, 1024, 768], P('dp'), may hold values from -6 to 6
- image_ids: int32 [16, 1024], P('dp'), may hold values from 0 to 3, never falling along the last dimension, each value on 1 to 512 neighbouring positions
- step_rates: float32 [2], replicated, may hold values from 0.2 to 0.6
- w_qkv: float32 [768, 3, 768], P('dp', None, 'tensor'), may hold values from -0.21875 to 0.21875
- w_out: float32 [768, 768], P('tensor', 'dp'), may hold values from -1.75 to 1.75
- w_up: float32 [768, 3072], P('dp', 'tensor'), may hold values from -0.4375 to 0.4375
- w_down: float32 [3072, 768], P('tensor', 'dp'), may hold values from -0.21875 to 0.21875
- norm_gains: float32 [2, 768], replicated, may hold values from 0.5 to 1.5
- row_biases: float32 [4, 768], replicated, may hold values from -1.8 to 1.8
- head_gains: float32 [2, 64], replicated, may hold values from 0.5 to 1.5
- query_bias: float32 [64], replicated, may hold values from -1.8 to 1.8
- qkv_bias: float32 [3, 768], P(None, 'tensor'), may hold values from -1.8 to 1.8
- hidden_bias: float32 [3072], P('tensor'), may hold values from -1.8 to 1.8
- mom_qkv: float32 [768, 3, 768], P('dp', None, 'tensor'), may hold values from -384 to 384
- mom_out: float32 [768, 768], P('tensor', 'dp'), may hold values from -384 to 14572.96
- mom_up: float32 [768, 3072], P('dp', 'tensor'), may hold values from -384 to 384
- mom_down: float32 [3072, 768], P('tensor', 'dp'), may hold values from -384 to 384
- mom_gains: float32 [2, 768], replicated, may hold values from -1024 to 1024
- mom_biases: float32 [4, 768], replicated, may hold values from -1536 to 1536
- mom_head_gains: float32 [2, 64], replicated, may hold values from -2048 to 2048
- mom_query_bias: float32 [64], replicated, may hold values from -3072 to 3072
- mom_qkv_bias: float32 [3, 768], P(None, 'tensor'), may hold values from -1536 to 1536
- mom_hidden_bias: float32 [3072], P('tensor'), may hold values from -384 to 384
Outputs:
- block_out: float32 [16, 1024, 768], P('dp')
- tokens_grad: float32 [16, 1024, 768], P('dp')
- grad_qkv: float32 [768, 3, 768], P('dp', None, 'tensor')
- grad_out: float32 [768, 768], P('tensor', 'dp')
- grad_up: float32 [768, 3072], P('dp', 'tensor')
- grad_down: float32 [3072, 768], P('tensor', 'dp')
- grad_gains: float32 [2, 768], replicated
- grad_biases: float32 [4, 768], replicated
- grad_head_gains: float32 [2, 64], replicated
- grad_query_bias: float32 [64], replicated
- grad_qkv_bias: float32 [3, 768], P(None, 'tensor')
- grad_hidden_bias: float32 [3072], P('tensor')
- next_mom_qkv: float32 [768, 3, 768], P('dp', None, 'tensor')
- next_mom_out: float32 [768, 768], P('tensor', 'dp')
- next_mom_up: float32 [768, 3072], P('dp', 'tensor')
- next_mom_down: float32 [3072, 768], P('tensor', 'dp')
- next_mom_gains: float32 [2, 768], replicated
- next_mom_biases: float32 [4, 768], replicated
- next_mom_head_gains: float32 [2, 64], replicated
- next_mom_query_bias: float32 [64], replicated
- next_mom_qkv_bias: float32 [3, 768], P(None, 'tensor')
- next_mom_hidden_bias: float32 [3072], P('tensor')
- new_w_qkv: float32 [768, 3, 768], P('dp', None, 'tensor')
- new_w_out: float32 [768, 768], P('tensor', 'dp')
- new_w_up: float32 [768, 3072], P('dp', 'tensor')
- new_w_down: float32 [3072, 768], P('tensor', 'dp')
- new_gains: float32 [2, 768], replicated
- new_biases: float32 [4, 768], replicated
- new_head_gains: float32 [2, 64], replicated
- new_query_bias: float32 [64], replicated
- new_qkv_bias: float32 [3, 768], P(None, 'tensor')
- new_hidden_bias: float32 [3072], P('tensor')
Inputs may be any that keep to these rules, and one draw needn't show every extreme that they name: `image_ids`: within each row of 1024 patches the ids never fall; each of the 4 images has 1 to 512 patches.
All inputs are finite; a program needn't handle non-finite values.
Results may differ from a plain program's by a relative error of at most 0.025.
Values may be sent and summed in bfloat16 or wider, within the bound.
No kernel may reach another device: no remote copies, remote signals or barrier semaphores. Data moves between devices by JAX's collectives and lax.ppermute only.
A program may use at most 256 MiB of HBM per device.

v0:
```python
import math

import jax
import jax.numpy as jnp
from jax import lax
from jax.sharding import PartitionSpec as P

D = 768
DH = 64
FF = 3072
NS_ITERS = 5


EPS = 1e-06
NS_A = 3.4445
NS_B = -4.775
NS_C = 2.0315
HIGHEST = lax.Precision.HIGHEST


def for_sending(x):
    return jax.tree.map(lambda a: a.astype(jnp.bfloat16) if a.dtype == jnp.float32 else a, x)


def from_root(block, axis, holder):
    block = jnp.where(lax.axis_index(axis) == holder, block, jnp.zeros_like(block))
    return lax.psum(block, axis)


def layer_norm(values_in, gain_row, shift_row):
    row_mean = jnp.mean(values_in, axis=-1, keepdims=True)
    centred = values_in - row_mean
    row_var = jnp.mean(centred * centred, axis=-1, keepdims=True)
    return centred * lax.rsqrt(row_var + EPS) * gain_row + shift_row


def gelu_tanh(values_in):
    return jax.nn.gelu(values_in, approximate=True)


def project_heads(raw_query, raw_keys, head_gains, query_bias):
    query_out = layer_norm(raw_query, head_gains[0], query_bias) * DH ** (-0.5)
    keys_out = layer_norm(raw_keys, head_gains[1], 0.0)
    return (query_out, keys_out)


def dense(left_in, right_in):
    return jnp.dot(left_in, right_in, preferred_element_type=jnp.float32)


def dense_exact(left_in, right_in):
    return jnp.dot(left_in, right_in, precision=HIGHEST)


def dense_tn(left_in, right_in):
    return lax.dot_general(
        left_in, right_in, (((0,), (0,)), ((), ())), preferred_element_type=jnp.float32
    )


def dense_nt(left_in, right_in):
    return lax.dot_general(
        left_in, right_in, (((1,), (1,)), ((), ())), preferred_element_type=jnp.float32
    )


def masked_scores(query_rows, keys_in, image_row, first_row, block_rows):
    scores = jnp.einsum("qhd,khd->hqk", query_rows, keys_in, preferred_element_type=jnp.float32)
    same_image = image_row[first_row : first_row + block_rows, None] == image_row[None, :]
    return jnp.where(same_image[None], scores, -1000000000.0)


def attend_forward(seq_item):
    query_in, keys_in, values, image_row = seq_item
    length = query_in.shape[0]
    block_rows = min(512, length)
    outputs = []
    totals = []
    for first_row in range(0, length, block_rows):
        scores = masked_scores(
            query_in[first_row : first_row + block_rows], keys_in, image_row, first_row, block_rows
        )
        row_max = jnp.max(scores, axis=-1, keepdims=True)
        row_total = row_max + jnp.log(jnp.sum(jnp.exp(scores - row_max), axis=-1, keepdims=True))
        attn_probs = jnp.exp(scores - row_total).astype(jnp.bfloat16)
        outputs.append(
            jnp.einsum("hqk,khd->qhd", attn_probs, values, preferred_element_type=jnp.float32)
        )
        totals.append(row_total)
    return (jnp.concatenate(outputs, 0), jnp.concatenate(totals, 1))


def attend_backward(seq_item):
    query_in, keys_in, values, image_row, totals, grad_mixed = seq_item
    length = query_in.shape[0]
    block_rows = min(512, length)
    grad_query_parts = []
    grad_keys = jnp.zeros(keys_in.shape, jnp.float32)
    grad_values = jnp.zeros(values.shape, jnp.float32)
    for first_row in range(0, length, block_rows):
        query_rows = query_in[first_row : first_row + block_rows]
        grad_rows = grad_mixed[first_row : first_row + block_rows]
        scores = masked_scores(query_rows, keys_in, image_row, first_row, block_rows)
        attn_probs = jnp.exp(scores - totals[:, first_row : first_row + block_rows])
        grad_probs = jnp.einsum(
            "qhd,khd->hqk", grad_rows, values, preferred_element_type=jnp.float32
        )
        grad_scores = attn_probs * (
            grad_probs - jnp.sum(grad_probs * attn_probs, axis=-1, keepdims=True)
        )
        grad_scores = grad_scores.astype(jnp.bfloat16)
        grad_query_parts.append(
            jnp.einsum("hqk,khd->qhd", grad_scores, keys_in, preferred_element_type=jnp.float32)
        )
        grad_keys = grad_keys + jnp.einsum(
            "hqk,qhd->khd", grad_scores, query_rows, preferred_element_type=jnp.float32
        )
        grad_values = grad_values + jnp.einsum(
            "hqk,qhd->khd",
            attn_probs.astype(jnp.bfloat16),
            grad_rows,
            preferred_element_type=jnp.float32,
        )
    return (jnp.concatenate(grad_query_parts, 0), grad_keys, grad_values)


def gram_branch(width):

    def gram_compute(iterate):
        part_cols = iterate[:, :width]
        return lax.dot_general(part_cols, part_cols, (((1,), (1,)), ((), ())), precision=HIGHEST)

    return gram_compute


def apply_branch(width, columns):

    def apply_compute(poly_term, iterate):
        product = dense_exact(poly_term, iterate[:, :width])
        return jnp.pad(product, ((0, 0), (0, columns - width)))

    return apply_compute


def newton_schulz(matrix, which, widths):
    columns = matrix.shape[1]
    gram_fns = [gram_branch(width) for width in widths]
    apply_fns = [apply_branch(width, columns) for width in widths]
    iterate = matrix
    for turn in range(NS_ITERS):
        gram_matrix = jax.tree.map(
            lambda part: part.astype(jnp.float32),
            lax.psum(for_sending(lax.switch(which, gram_fns, iterate)), "tensor"),
        )
        if turn == 0:
            root = jnp.sqrt(jnp.trace(gram_matrix)) + 1e-07
            gram_matrix = gram_matrix / (root * root)
        poly_term = NS_B * gram_matrix + NS_C * dense_exact(gram_matrix, gram_matrix)
        iterate = NS_A * iterate + lax.switch(which, apply_fns, poly_term, iterate)
        if turn == 0:
            iterate = iterate / root
    return iterate


def widen(matrix, columns):
    return jnp.pad(matrix, ((0, 0), (0, columns - matrix.shape[1])))


def body(
    tokens,
    cotangent,
    image_ids,
    step_rates,
    w_qkv,
    w_out,
    w_up,
    w_down,
    norm_gains,
    row_biases,
    head_gains,
    query_bias,
    qkv_bias,
    hidden_bias,
    mom_qkv,
    mom_out,
    mom_up,
    mom_down,
    mom_gains,
    mom_biases,
    mom_head_gains,
    mom_query_bias,
    mom_qkv_bias,
    mom_hidden_bias,
):
    dp_count = lax.axis_size("dp")
    tensor_count = lax.axis_size("tensor")
    seq_count, length, model_width = tokens.shape
    row_count = seq_count * length
    shard_rows = w_qkv.shape[0]
    half_width = w_qkv.shape[2]
    hidden_part = w_up.shape[1]
    heads_part = half_width // DH
    widths = [3 * half_width, half_width, hidden_part, hidden_part]
    full_qkv, full_out, full_up, full_down = (
        lax.all_gather(w_qkv.astype(jnp.bfloat16), "dp", axis=0, tiled=True),
        lax.all_gather(w_out.astype(jnp.bfloat16), "dp", axis=1, tiled=True),
        lax.all_gather(w_up.astype(jnp.bfloat16), "dp", axis=0, tiled=True),
        lax.all_gather(w_down.astype(jnp.bfloat16), "dp", axis=1, tiled=True),
    )
    qkv_matrix = full_qkv.reshape(model_width, 3 * half_width)
    flat_in = tokens.reshape(row_count, model_width).astype(jnp.float32)
    normed_f, norm_one_pull = jax.vjp(layer_norm, flat_in, norm_gains[0], row_biases[0])
    normed_one = normed_f.astype(jnp.bfloat16)
    raw_qkv = dense(normed_one, qkv_matrix) + qkv_bias.reshape(3 * half_width)
    raw_qkv = raw_qkv.reshape(row_count, 3, heads_part, DH)
    (query_f, keys_f), head_pull = jax.vjp(
        project_heads, raw_qkv[:, 0], raw_qkv[:, 1], head_gains, query_bias
    )
    seq_shape = (seq_count, length, heads_part, DH)
    query_low = query_f.astype(jnp.bfloat16).reshape(seq_shape)
    keys_low = keys_f.astype(jnp.bfloat16).reshape(seq_shape)
    values_low = raw_qkv[:, 2].astype(jnp.bfloat16).reshape(seq_shape)
    mixed_f, totals = lax.map(attend_forward, (query_low, keys_low, values_low, image_ids))
    mixed_heads = mixed_f.reshape(row_count, half_width).astype(jnp.bfloat16)
    attn_out = lax.psum(dense(mixed_heads, full_out), "tensor") + row_biases[1]
    residual = flat_in + attn_out
    normed_two_f, norm_two_pull = jax.vjp(layer_norm, residual, norm_gains[1], row_biases[2])
    normed_two = normed_two_f.astype(jnp.bfloat16)
    pre_act = dense(normed_two, full_up) + hidden_bias
    act_f, gelu_pull = jax.vjp(gelu_tanh, pre_act)
    act_out = act_f.astype(jnp.bfloat16)
    mlp_out = (
        lax.psum(dense(act_out, full_down).astype(jnp.bfloat16), "tensor").astype(jnp.float32)
        + row_biases[3]
    )
    block_out = (residual + mlp_out).reshape(tokens.shape)
    grad_y = cotangent.reshape(row_count, model_width).astype(jnp.float32)
    grad_y_low = grad_y.astype(jnp.bfloat16)
    grad_down_local = dense_tn(act_out, grad_y_low)
    (grad_pre,) = gelu_pull(dense_nt(grad_y_low, full_down))
    grad_pre_low = grad_pre.astype(jnp.bfloat16)
    grad_up_local = dense_tn(normed_two, grad_pre_low)
    grad_normed_two = lax.psum(dense_nt(grad_pre_low, full_up), "tensor")
    grad_resid_ln, grad_gain_two, grad_shift_two = norm_two_pull(grad_normed_two)
    grad_resid = grad_y + grad_resid_ln
    grad_resid_low = grad_resid.astype(jnp.bfloat16)
    grad_out_local = dense_tn(mixed_heads, grad_resid_low)
    grad_mixed = dense_nt(grad_resid_low, full_out).astype(jnp.bfloat16).reshape(seq_shape)
    grad_query, grad_keys, grad_values = lax.map(
        attend_backward, (query_low, keys_low, values_low, image_ids, totals, grad_mixed)
    )
    head_shape = (row_count, heads_part, DH)
    grad_raw_query, grad_raw_keys, grad_head_local, grad_qshift_local = head_pull(
        (grad_query.reshape(head_shape), grad_keys.reshape(head_shape))
    )
    grad_raw = jnp.stack(
        [grad_raw_query, grad_raw_keys, grad_values.reshape(head_shape)], axis=1
    ).reshape(row_count, 3 * half_width)
    grad_qkv_bias_local = jnp.sum(grad_raw, axis=0).reshape(3, half_width)
    grad_raw_low = grad_raw.astype(jnp.bfloat16)
    grad_qkv_local = dense_tn(normed_one, grad_raw_low).reshape(model_width, 3, half_width)
    grad_normed_one = lax.psum(
        dense_nt(grad_raw_low, qkv_matrix).astype(jnp.bfloat16), "tensor"
    ).astype(jnp.float32)
    grad_flat_ln, grad_gain_one, grad_shift_one = norm_one_pull(grad_normed_one)
    tokens_grad = (grad_resid + grad_flat_ln).reshape(tokens.shape)
    grad_qkv, grad_out, grad_up, grad_down = (
        lax.psum_scatter(grad_qkv_local, "dp", scatter_dimension=0, tiled=True),
        lax.psum_scatter(grad_out_local, "dp", scatter_dimension=1, tiled=True),
        lax.psum_scatter(grad_up_local, "dp", scatter_dimension=0, tiled=True),
        lax.psum_scatter(grad_down_local, "dp", scatter_dimension=1, tiled=True),
    )
    own_mask = (jnp.arange(tensor_count) == lax.axis_index("tensor")).astype(jnp.float32)
    gains_local = 0.5 * jnp.stack([grad_gain_one, grad_gain_two])
    biases_local = 0.5 * jnp.stack(
        [grad_shift_one, jnp.sum(grad_resid, axis=0), grad_shift_two, jnp.sum(grad_y, axis=0)]
    )
    qkv_bias_spread = own_mask[None, :, None] * grad_qkv_bias_local[:, None, :]
    hidden_spread = own_mask[:, None] * jnp.sum(grad_pre, axis=0)[None, :]
    summed = lax.psum(
        (
            gains_local,
            biases_local,
            grad_head_local,
            grad_qshift_local,
            qkv_bias_spread,
            hidden_spread,
        ),
        ("dp", "tensor"),
    )
    grad_gains = summed[0]
    grad_biases = summed[1]
    grad_head_gains = summed[2]
    grad_query_bias = summed[3]
    grad_qkv_bias = jnp.sum(summed[4] * own_mask[None, :, None], axis=1)
    grad_hidden_bias = jnp.sum(summed[5] * own_mask[:, None], axis=0)
    next_mom_qkv = 0.5 * mom_qkv + grad_qkv
    next_mom_out = 0.5 * mom_out + grad_out
    next_mom_up = 0.5 * mom_up + grad_up
    next_mom_down = 0.5 * mom_down + grad_down
    row_mats = (
        next_mom_qkv.reshape(shard_rows, 3 * half_width),
        next_mom_out.T,
        next_mom_up,
        next_mom_down.T,
    )
    dp_index = lax.axis_index("dp")
    owned = dp_index % 4
    gathered = (
        lax.all_gather(row_mats[0].astype(jnp.bfloat16), "dp", axis=0, tiled=True).astype(
            jnp.float32
        ),
        lax.all_gather(row_mats[1].astype(jnp.bfloat16), "dp", axis=0, tiled=True).astype(
            jnp.float32
        ),
        lax.all_gather(row_mats[2].astype(jnp.bfloat16), "dp", axis=0, tiled=True).astype(
            jnp.float32
        ),
        lax.all_gather(row_mats[3].astype(jnp.bfloat16), "dp", axis=0, tiled=True).astype(
            jnp.float32
        ),
    )
    all_moments = jnp.stack([widen(whole, hidden_part) for whole in gathered])
    own_matrix = lax.dynamic_index_in_dim(all_moments, owned, 0, keepdims=False)
    orthogonal = newton_schulz(own_matrix, owned, widths)
    own_rows = []
    for owner in range(4):
        full_result = from_root(for_sending(orthogonal[:, : widths[owner]]), "dp", owner)
        own_rows.append(lax.dynamic_slice_in_dim(full_result, dp_index * shard_rows, shard_rows, 0))
    rate_muon = step_rates[0]
    new_w_qkv = w_qkv - rate_muon * (0.2 * math.sqrt(max(D, 3 * D))) * own_rows[0][
        :, : 3 * half_width
    ].reshape(shard_rows, 3, half_width)
    new_w_out = w_out - rate_muon * (0.2 * math.sqrt(D)) * own_rows[1][:, :half_width].T
    new_w_up = w_up - rate_muon * (0.2 * math.sqrt(max(D, FF))) * own_rows[2][:, :hidden_part]
    new_w_down = w_down - rate_muon * (0.2 * math.sqrt(max(D, FF))) * own_rows[3][:, :hidden_part].T
    rate_vector = step_rates[1] / math.sqrt(row_count * dp_count)
    next_mom_gains = 0.5 * mom_gains + grad_gains
    next_mom_biases = 0.5 * mom_biases + grad_biases
    next_mom_head_gains = 0.5 * mom_head_gains + grad_head_gains
    next_mom_query_bias = 0.5 * mom_query_bias + grad_query_bias
    next_mom_qkv_bias = 0.5 * mom_qkv_bias + grad_qkv_bias
    next_mom_hidden_bias = 0.5 * mom_hidden_bias + grad_hidden_bias
    new_gains = norm_gains - rate_vector * next_mom_gains
    new_biases = row_biases - rate_vector * next_mom_biases
    new_head_gains = head_gains - rate_vector * next_mom_head_gains
    new_query_bias = query_bias - rate_vector * next_mom_query_bias
    new_qkv_bias = qkv_bias - rate_vector * next_mom_qkv_bias
    new_hidden_bias = hidden_bias - rate_vector * next_mom_hidden_bias
    return (
        block_out,
        tokens_grad,
        grad_qkv,
        grad_out,
        grad_up,
        grad_down,
        grad_gains,
        grad_biases,
        grad_head_gains,
        grad_query_bias,
        grad_qkv_bias,
        grad_hidden_bias,
        next_mom_qkv,
        next_mom_out,
        next_mom_up,
        next_mom_down,
        next_mom_gains,
        next_mom_biases,
        next_mom_head_gains,
        next_mom_query_bias,
        next_mom_qkv_bias,
        next_mom_hidden_bias,
        new_w_qkv,
        new_w_out,
        new_w_up,
        new_w_down,
        new_gains,
        new_biases,
        new_head_gains,
        new_query_bias,
        new_qkv_bias,
        new_hidden_bias,
    )


def solution(mesh):
    return jax.shard_map(
        body,
        mesh=mesh,
        in_specs=(
            P("dp", None, None),
            P("dp", None, None),
            P("dp", None),
            P(),
            P("dp", None, "tensor"),
            P("tensor", "dp"),
            P("dp", "tensor"),
            P("tensor", "dp"),
            P(),
            P(),
            P(),
            P(),
            P(None, "tensor"),
            P("tensor"),
            P("dp", None, "tensor"),
            P("tensor", "dp"),
            P("dp", "tensor"),
            P("tensor", "dp"),
            P(),
            P(),
            P(),
            P(),
            P(None, "tensor"),
            P("tensor"),
        ),
        out_specs=(
            P("dp", None, None),
            P("dp", None, None),
            P("dp", None, "tensor"),
            P("tensor", "dp"),
            P("dp", "tensor"),
            P("tensor", "dp"),
            P(),
            P(),
            P(),
            P(),
            P(None, "tensor"),
            P("tensor"),
            P("dp", None, "tensor"),
            P("tensor", "dp"),
            P("dp", "tensor"),
            P("tensor", "dp"),
            P(),
            P(),
            P(),
            P(),
            P(None, "tensor"),
            P("tensor"),
            P("dp", None, "tensor"),
            P("tensor", "dp"),
            P("dp", "tensor"),
            P("tensor", "dp"),
            P(),
            P(),
            P(),
            P(),
            P(None, "tensor"),
            P("tensor"),
        ),
        check_vma=False,
    )
```

profile of v0, /device:TPU:0, one launch (start us, length us, event | category | flops | bytes accessed | tf_op | source)
XLA Modules:
  0.0 1792.6 jit_solution(1700993021410551867)
XLA Ops:
  16.7 46.6 %all_gather.25 = bf16[384,768]{0,1:T(8,128)(2,1)S(1)} all-gather(bf16[384,48]{0,1:T(8,128)(2,1)S(1)} %convert_element_type.215), channel_id=1, replica_groups=mesh['dp'=16,'tensor'=2] {'dp'}, dimensions={1}, use_global_device_ids=true | all-gather | bytes 626688 | tf_op jit(solution)/shard_map/all_gather | solution.py:206
  121.9 20.6 %all-reduce.26.cloned.1.call-done = f32[1024,768]{1,0:T(8,128)} async-done(((f32[1024,768]{1,0:T(8,128)}), f32[1024,768]{1,0:T(8,128)}) %all-reduce.26.cloned.1.call-update) | async-done | bytes 3145744 | tf_op jit(solution)/shard_map/psum | solution.py:225
  145.8 63.4 %all-gather.9.cloned.1.call-done = bf16[768,1536]{1,0:T(8,128)(2,1)} async-done(((bf16[48,1536]{1,0:T(8,128)(2,1)}), bf16[768,1536]{1,0:T(8,128)(2,1)}) %all-gather.9.cloned.1.call-update) | async-done | bytes 2359312 | tf_op jit(solution)/shard_map/all_gather | solution.py:207
  216.1 57.0 %all-gather.11.cloned.1.call-done = bf16[1536,768]{0,1:T(8,128)(2,1)} async-done(((bf16[1536,48]{0,1:T(8,128)(2,1)}), bf16[1536,768]{0,1:T(8,128)(2,1)}) %all-gather.11.cloned.1.call-update) | async-done | bytes 2359312 | tf_op jit(solution)/shard_map/all_gather | solution.py:208
  289.7 20.7 %all-reduce.28.cloned.1.call-done = f32[1024,768]{1,0:T(8,128)} async-done(((f32[1024,768]{1,0:T(8,128)}), f32[1024,768]{1,0:T(8,128)}) %all-reduce.28.cloned.1.call-update) | async-done | bytes 3145744 | tf_op jit(solution)/shard_map/psum | solution.py:243
  411.8 112.1 %reduce-scatter.5.cloned.1.call-done = f32[48,3,384]{2,0,1:T(8,128)} async-done(((f32[768,3,384]{2,0,1:T(8,128)}), f32[48,3,384]{2,0,1:T(8,128)}) %reduce-scatter.5.cloned.1.call-update) | async-done | bytes 221200 | tf_op jit(solution)/shard_map/reduce_scatter | solution.py:268
  526.4 140.7 %reduce-scatter.11.cloned.1.call-done = f32[1536,48]{0,1:T(8,128)} async-done(((f32[1536,768]{0,1:T(8,128)}), f32[1536,48]{0,1:T(8,128)}) %reduce-scatter.11.cloned.1.call-update) | async-done | bytes 294928 | tf_op jit(solution)/shard_map/reduce_scatter | solution.py:271
  669.0 141.2 %reduce-scatter.9.cloned.1.call-done = f32[48,1536]{1,0:T(8,128)} async-done(((f32[768,1536]{1,0:T(8,128)}), f32[48,1536]{1,0:T(8,128)}) %reduce-scatter.9.cloned.1.call-update) | async-done | bytes 294928 | tf_op jit(solution)/shard_map/reduce_scatter | solution.py:270
  812.0 127.3 %reduce-scatter.7.cloned.1.call-done = f32[384,48]{0,1:T(8,128)} async-done(((f32[384,768]{0,1:T(8,128)}), f32[384,48]{0,1:T(8,128)}) %reduce-scatter.7.cloned.1.call-update) | async-done | bytes 73744 | tf_op jit(solution)/shard_map/reduce_scatter | solution.py:269
  940.8 43.5 %all_gather.29 = bf16[768,384]{1,0:T(8,128)(2,1)S(1)} all-gather(bf16[48,384]{1,0:T(8,128)(2,1)S(1)} %get-tuple-element.425), channel_id=1, replica_groups=mesh['dp'=16,'tensor'=2] {'dp'}, dimensions={0}, use_global_device_ids=true | all-gather | bytes 626688 | tf_op jit(solution)/shard_map/all_gather | solution.py:313
  1004.5 61.2 %all-gather.17.cloned.1.call-done = bf16[768,1536]{1,0:T(8,128)(2,1)} async-done(((bf16[48,1536]{1,0:T(8,128)(2,1)}), bf16[768,1536]{1,0:T(8,128)(2,1)}) %all-gather.17.cloned.1.call-update) | async-done | bytes 2359312 | tf_op jit(solution)/shard_map/all_gather | solution.py:319
  1065.7 63.8 %all-gather.15.cloned.1.call-done = bf16[768,1536]{1,0:T(8,128)(2,1)} async-done(((bf16[48,1536]{1,0:T(8,128)(2,1)}), bf16[768,1536]{1,0:T(8,128)(2,1)}) %all-gather.15.cloned.1.call-update) | async-done | bytes 2359312 | tf_op jit(solution)/shard_map/all_gather | solution.py:316
  1134.1 20.8 %conditional.10 = (bf16[768,768]{1,0:T(8,128)(2,1)S(1)}) conditional(s32[]{:T(128)} %clamp.2, f32[768,1536]{1,0:T(8,128)} %convert_bitcast_fusion.1, f32[768,1536]{1,0:T(8,128)} %convert_bitcast_fusion.1, f32[768,1536]{1,0:T(8,128)} %convert_bitcast_fusion.1, f32[768,1536]{1,0:T(8,128)} %convert_bitcast_fusion.1), branch_computations={%region_49.50_spmd, %region_50.51_spmd, %region_51.52_spmd, %regio... | conditional | flops 10871635968 | bytes 5898248 | solution.py:153
  1209.3 28.3 %conditional.12 = (bf16[768,768]{1,0:T(8,128)(2,1)S(1)}) conditional(s32[]{:T(128)} %clamp.2, f32[768,1536]{1,0:T(8,128)S(1)} %add_divide_fusion, f32[768,1536]{1,0:T(8,128)S(1)} %add_divide_fusion, f32[768,1536]{1,0:T(8,128)S(1)} %add_divide_fusion, f32[768,1536]{1,0:T(8,128)S(1)} %add_divide_fusion), branch_computations={%region_59.60_spmd, %region_60.61_spmd, %region_61.62_spmd, %regio... | conditional | flops 10871635968 | bytes 5898248 | solution.py:153
  1238.7 22.2 %all-reduce.32.cloned.1.call-done = bf16[768,768]{1,0:T(8,128)(2,1)} async-done(((bf16[768,768]{1,0:T(8,128)(2,1)}), bf16[768,768]{1,0:T(8,128)(2,1)}) %all-reduce.32.cloned.1.call-update) | async-done | bytes 1179664 | tf_op jit(solution)/shard_map/psum | solution.py:153
  1264.2 22.9 %conditional.13 = (f32[768,1536]{1,0:T(8,128)}) conditional(s32[]{:T(128)} %clamp.2, (f32[768,1536]{1,0:T(8,128)}, f32[768,768]{1,0:T(8,128)S(1)}) %tuple.276, (f32[768,1536]{1,0:T(8,128)}, f32[768,768]{1,0:T(8,128)S(1)}) %tuple.277, (f32[768,768]{1,0:T(8,128)S(1)}, f32[768,1536]{1,0:T(8,128)}) %tuple.278, ...), branch_computations={%region_64.65_spmd, %region_65.66_spmd, %region_66.67_spmd, %regio... | conditional | flops 10871635968 | bytes 17694732 | solution.py:159
  1294.1 28.3 %conditional.14 = (bf16[768,768]{1,0:T(8,128)(2,1)S(1)}) conditional(s32[]{:T(128)} %clamp.2, f32[768,1536]{1,0:T(8,128)S(1)} %multiply_add_fusion.2, f32[768,1536]{1,0:T(8,128)S(1)} %multiply_add_fusion.2, f32[768,1536]{1,0:T(8,128)S(1)} %multiply_add_fusion.2, f32[768,1536]{1,0:T(8,128)S(1)} %multiply_add_fusion.2), branch_computations={%region_68.69_spmd, %region_69.70_spmd, %region_70.71_spmd, %regio... | conditional | flops 10871635968 | bytes 5898248 | solution.py:153
  1323.5 22.1 %all-reduce.34.cloned.1.call-done = bf16[768,768]{1,0:T(8,128)(2,1)} async-done(((bf16[768,768]{1,0:T(8,128)(2,1)}), bf16[768,768]{1,0:T(8,128)(2,1)}) %all-reduce.34.cloned.1.call-update) | async-done | bytes 1179664 | tf_op jit(solution)/shard_map/psum | solution.py:153
  1348.8 22.9 %conditional.15 = (f32[768,1536]{1,0:T(8,128)}) conditional(s32[]{:T(128)} %clamp.2, (f32[768,1536]{1,0:T(8,128)}, f32[768,768]{1,0:T(8,128)S(1)}) %tuple.268, (f32[768,1536]{1,0:T(8,128)}, f32[768,768]{1,0:T(8,128)S(1)}) %tuple.269, (f32[768,768]{1,0:T(8,128)S(1)}, f32[768,1536]{1,0:T(8,128)}) %tuple.270, ...), branch_computations={%region_73.74_spmd, %region_74.75_spmd, %region_75.76_spmd, %regio... | conditional | flops 10871635968 | bytes 17694732 | solution.py:159
  1449.7 28.1 %conditional.18 = (bf16[768,768]{1,0:T(8,128)(2,1)S(1)}) conditional(s32[]{:T(128)} %clamp.2, f32[768,1536]{1,0:T(8,128)S(1)} %multiply_add_fusion, f32[768,1536]{1,0:T(8,128)S(1)} %multiply_add_fusion, f32[768,1536]{1,0:T(8,128)S(1)} %multiply_add_fusion, f32[768,1536]{1,0:T(8,128)S(1)} %multiply_add_fusion), branch_computations={%region_86.87_spmd, %region_87.88_spmd, %region_88.89_spmd, %regio... | conditional | flops 10871635968 | bytes 5898248 | solution.py:153
  1478.9 31.1 %all-reduce.40.cloned.1.call-done = (bf16[1024,768]{1,0:T(8,128)(2,1)}, bf16[1024,768]{1,0:T(8,128)(2,1)}, bf16[768,768]{1,0:T(8,128)(2,1)}) async-done(((bf16[1024,768]{1,0:T(8,128)(2,1)}, bf16[1024,768]{1,0:T(8,128)(2,1)}, bf16[768,768]{1,0:T(8,128)(2,1)}), (bf16[1024,768]{1,0:T(8,128)(2,1)}, bf16[1024,768]{1,0:T(8,128)(2,1)}, bf16[768,768]{1,0:T(8,128)(2,1)})) %all-reduce.40.cloned.1.call-update) | async-done | bytes 4325392 | tf_op jit(solution)/shard_map/psum | solution.py:233
  1513.3 26.7 %conditional.19 = (f32[768,1536]{1,0:T(8,128)}) conditional(s32[]{:T(128)} %clamp.2, (f32[768,1536]{1,0:T(8,128)S(1)}, f32[768,768]{1,0:T(8,128)S(1)}) %tuple.272, (f32[768,1536]{1,0:T(8,128)S(1)}, f32[768,768]{1,0:T(8,128)S(1)}) %tuple.273, (f32[768,768]{1,0:T(8,128)S(1)}, f32[768,1536]{1,0:T(8,128)S(1)}) %tuple.274, ...), branch_computations={%region_91.92_spmd, %region_92.93_spmd, %region_93.94_spmd, %regio... | conditional | flops 10871635968 | bytes 17694732 | solution.py:159
  1567.1 43.2 %all-reduce.14 = (f32[2,768]{1,0:T(2,128)S(1)}, f32[4,768]{1,0:T(4,128)S(1)}, f32[2,64]{1,0:T(2,128)S(1)}, f32[64]{0:T(128)S(1)}, f32[3,2,384]{2,1,0:T(2,128)S(1)}, /*index=5*/f32[2,1536]{1,0:T(2,128)S(1)}) all-reduce(f32[2,768]{1,0:T(2,128)S(1)} %maximum_multiply_fusion.2, ...), channel_id=1, replica_groups=mesh['dp'=16,'tensor'=2] {'dp','tensor'}, use_global_device_ids=true, to_apply=%region_32.33 | all-reduce | flops 10176 | bytes 81408 | tf_op jit(solution)/shard_map/psum | solution.py:280
  1617.6 160.2 %all-reduce.38.cloned.1.call-done = (bf16[768,1152]{1,0:T(8,128)(2,1)}, bf16[768,384]{1,0:T(8,128)(2,1)}, bf16[768,1536]{1,0:T(8,128)(2,1)}, bf16[768,1536]{1,0:T(8,128)(2,1)}) async-done(((bf16[768,1152]{1,0:T(8,128)(2,1)}, bf16[768,384]{1,0:T(8,128)(2,1)}, bf16[768,1536]{1,0:T(8,128)(2,1)}, bf16[768,1536]{1,0:T(8,128)(2,1)}), (bf16[768,1152]{1,0:T(8,128)(2,1)}, bf16[768,384]{1,0:T(8,128)(2,1)}, ...) | async-done | bytes 7077904 | tf_op jit(solution)/shard_map/psum | solution.py:27
  (461 shorter events, 542.1 us)
Async XLA Ops:
  7.2 67.1 %all-gather.7.cloned.1.call-start = ((), (), s32[]{:S(2)}) async-start(), calls=%async_computation.4 | async-start | bytes 1880064 | tf_op jit(solution)/shard_map/all_gather | solution.py:205
  9.0 133.5 %all-reduce.26.cloned.1.call-start = ((), (), s32[]{:S(2)}) async-start(), calls=%async_computation.5 | async-start | bytes 6291456 | tf_op jit(solution)/shard_map/psum | solution.py:225
  11.4 302.5 %copy-start.75 = (f32[768]{0:T(1024)}, f32[768]{0:T(1024)S(1)}, u32[]{:S(2)}) copy-start(f32[768]{0:T(1024)S(1)} %get-tuple-element.392) | copy-start | bytes 9220
  11.4 370.3 %copy-start.70 = (f32[768]{0:T(1024)}, f32[768]{0:T(1024)S(1)}, u32[]{:S(2)}) copy-start(f32[768]{0:T(1024)S(1)} %get-tuple-element.393) | copy-start | bytes 9220
  16.1 365.6 %copy-start.67 = (f32[1024]{0:T(1024)}, f32[1024]{0:T(1024)S(1)}, u32[]{:S(2)}) copy-start(f32[1024]{0:T(1024)S(1)} %broadcast_multiply_fusion.5) | copy-start | bytes 12292
  120.3 88.9 %all-gather.9.cloned.1.call-start = ((), (), s32[]{:S(2)}) async-start(), calls=%async_computation.6 | async-start | bytes 2506752 | tf_op jit(solution)/shard_map/all_gather | solution.py:207
  121.1 152.0 %all-gather.11.cloned.1.call-start = ((), (), s32[]{:S(2)}) async-start(), calls=%async_computation.7 | async-start | bytes 2506752 | tf_op jit(solution)/shard_map/all_gather | solution.py:208
  121.8 188.6 %all-reduce.28.cloned.1.call-start = ((), (), s32[]{:S(2)}) async-start(), calls=%async_computation.8 | async-start | bytes 6291456 | tf_op jit(solution)/shard_map/psum | solution.py:243
  288.5 235.4 %reduce-scatter.5.cloned.1.call-start = ((), (), s32[]{:S(2)}) async-start(), calls=%async_computation.9 | async-start | bytes 3760128 | tf_op jit(solution)/shard_map/reduce_scatter | solution.py:268
  388.0 279.1 %reduce-scatter.11.cloned.1.call-start = ((), (), s32[]{:S(2)}) async-start(), calls=%async_computation.12 | async-start | bytes 5013504 | tf_op jit(solution)/shard_map/reduce_scatter | solution.py:271
  397.6 412.6 %reduce-scatter.9.cloned.1.call-start = ((), (), s32[]{:S(2)}) async-start(), calls=%async_computation.11 | async-start | bytes 5013504 | tf_op jit(solution)/shard_map/reduce_scatter | solution.py:270
  406.0 261.1 %copy-start.65 = (f32[1536,48]{0,1:T(8,128)S(1)}, f32[1536,48]{0,1:T(8,128)}, u32[]{:S(2)}) copy-start(f32[1536,48]{0,1:T(8,128)} %param.81) | copy-start | bytes 884740
  406.0 533.3 %reduce-scatter.7.cloned.1.call-start = ((), (), s32[]{:S(2)}) async-start(), calls=%async_computation.10 | async-start | bytes 1253376 | tf_op jit(solution)/shard_map/reduce_scatter | solution.py:269
  411.8 398.4 %copy-start.66 = (f32[48,1536]{1,0:T(8,128)S(1)}, f32[48,1536]{1,0:T(8,128)}, u32[]{:S(2)}) copy-start(f32[48,1536]{1,0:T(8,128)} %param.80) | copy-start | bytes 884740
  411.8 527.5 %copy-start.69 = (f32[384,48]{0,1:T(8,128)S(1)}, f32[384,48]{0,1:T(8,128)}, u32[]{:S(2)}) copy-start(f32[384,48]{0,1:T(8,128)} %param.79) | copy-start | bytes 221188
  411.8 589.6 %all-gather.13.cloned.1.call-start = ((), (), s32[]{:S(2)}) async-start(), calls=%async_computation.13 | async-start | bytes 1880064 | tf_op jit(solution)/shard_map/all_gather | solution.py:310
  526.3 539.3 %all-gather.17.cloned.1.call-start = ((), (), s32[]{:S(2)}) async-start(), calls=%async_computation.15 | async-start | bytes 2506752 | tf_op jit(solution)/shard_map/all_gather | solution.py:319
  668.9 460.6 %all-gather.15.cloned.1.call-start = ((), (), s32[]{:S(2)}) async-start(), calls=%async_computation.14 | async-start | bytes 2506752 | tf_op jit(solution)/shard_map/all_gather | solution.py:316
  812.0 364.8 %all-reduce.30.cloned.1.call-start = ((), (), s32[]{:S(2)}) async-start(), calls=%async_computation.16 | async-start | bytes 2359296 | tf_op jit(solution)/shard_map/psum | solution.py:153
  1156.0 104.9 %all-reduce.32.cloned.1.call-start = ((), (), s32[]{:S(2)}) async-start(), calls=%async_computation.17 | async-start | bytes 2359296 | tf_op jit(solution)/shard_map/psum | solution.py:153
  1238.6 107.0 %all-reduce.34.cloned.1.call-start = ((), (), s32[]{:S(2)}) async-start(), calls=%async_computation.18 | async-start | bytes 2359296 | tf_op jit(solution)/shard_map/psum | solution.py:153
  1323.5 101.2 %all-reduce.36.cloned.1.call-start = ((), (), s32[]{:S(2)}) async-start(), calls=%async_computation.19 | async-start | bytes 2359296 | tf_op jit(solution)/shard_map/psum | solution.py:153
  1393.1 116.9 %all-reduce.40.cloned.1.call-start = ((), (), s32[]{:S(2)}) async-start(), calls=%async_computation.21 | async-start | bytes 8650752 | tf_op jit(solution)/shard_map/psum | solution.py:233
  1478.9 299.0 %all-reduce.38.cloned.1.call-start = ((), (), s32[]{:S(2)}) async-start(), calls=%async_computation.20 | async-start | bytes 14155776 | tf_op jit(solution)/shard_map/psum | solution.py:27
  (129 other events, 2752.4 us)
Sparse Core Ops, SparseCore 0:
  11.3 63.0 all-gather.6
  120.4 21.9 all-reduce.25
  145.8 63.3 all-gather.8
  212.5 60.5 all-gather.10
  288.6 21.6 all-reduce.27
  388.2 135.7 reduce-scatter.4
  529.6 137.4 reduce-scatter.10
  672.9 137.2 reduce-scatter.8
  815.5 123.7 reduce-scatter.6
  942.5 58.7 all-gather.12
  1004.7 60.8 all-gather.16
  1068.9 60.5 all-gather.14
  1156.1 20.5 all-reduce.29
  1238.7 22.1 all-reduce.31
  1323.6 21.9 all-reduce.33
  1393.2 31.3 all-reduce.35
  1479.0 30.9 all-reduce.39
  1550.6 227.2 all-reduce.37
where the time goes:
time: 1800 us; the launch traced here: 1790 us
  waiting for transfers between devices  1090 us (61%)
  matrix products  248 us (14%)
  blocking collectives  133 us (7%)
  other arithmetic  122 us (7%)
  loops' own time  96.5 us (5%)
  local copies, waits for them, and re-layouts  61.2 us (3%)
  starting transfers between devices  24.5 us (1%)
  between operations  19.6 us (1%)
    psum x1, waiting for transfers between devices, from_root(): return lax.psum(block, axis)  160 us
    reduce_scatter x1, waiting for transfers between devices, body(): lax.psum_scatter(grad_up_local, 'dp', scatter_dimension=0, tiled=True)  141 us
    reduce_scatter x1, waiting for transfers between devices, body(): lax.psum_scatter(grad_down_local, 'dp', scatter_dimension=1, tiled=True)  141 us
    reduce_scatter x1, waiting for transfers between devices, body(): lax.psum_scatter(grad_out_local, 'dp', scatter_dimension=1, tiled=True)  127 us
    reduce_scatter x1, waiting for transfers between devices, body(): lax.psum_scatter(grad_qkv_local, 'dp', scatter_dimension=0, tiled=True)  112 us
    dot_general x10, matrix products, dense_exact(): return jnp.dot(left_in, right_in, precision=HIGHEST)  76.7 us
    another operation x5, loops' own time, newton_schulz(): lax.switch(which, gram_fns, iterate)  64.5 us
    all_gather x1, waiting for transfers between devices, body(): lax.all_gather(row_mats[2].astype(jnp.bfloat16), 'dp', axis=0, tiled=True)  63.8 us
  transfers between devices with their start and end apart: 18, of which 18 were waited for; matrix products, arithmetic and copies ran while one was open for 5% of the time, Pallas kernels for 0%

commit v1 on v0

--- a/solution.py
+++ b/solution.py
@@ -1,8 +1,11 @@
+import functools
 import math
 
 import jax
 import jax.numpy as jnp
 from jax import lax
+from jax.experimental import pallas as pl
+from jax.experimental.pallas import tpu as pltpu
 from jax.sharding import PartitionSpec as P
 
 D = 768
@@ -15,16 +18,299 @@
 NS_A = 3.4445
 NS_B = -4.775
 NS_C = 2.0315
-HIGHEST = lax.Precision.HIGHEST
-
-
-def for_sending(x):
-    return jax.tree.map(lambda a: a.astype(jnp.bfloat16) if a.dtype == jnp.float32 else a, x)
-
-
-def from_root(block, axis, holder):
-    block = jnp.where(lax.axis_index(axis) == holder, block, jnp.zeros_like(block))
-    return lax.psum(block, axis)
+BF = jnp.bfloat16
+F32 = jnp.float32
+BOTH = ("dp", "tensor")
+
+
+def exchange(block, flip_zero, flip_one):
+    pairs = []
+    for place in range(lax.axis_size("dp")):
+        for core, flip in enumerate((flip_zero, flip_one)):
+            pairs.append((2 * place + core, 2 * (place ^ flip) + core))
+    return lax.ppermute(block, BOTH, pairs)
+
+
+def swap_cores(block):
+    return lax.ppermute(block, "tensor", [(0, 1), (1, 0)])
+
+
+def pick(stack, index):
+    return lax.dynamic_index_in_dim(stack, index, 0, keepdims=False)
+
+
+def gather_rows(block):
+    if lax.axis_size("dp") != 16:
+        return lax.all_gather(block, "dp", axis=0, tiled=True)
+    rows, columns = block.shape
+    place = lax.axis_index("dp")
+    inner, outer = place % 4, place // 4
+    first = lax.axis_index("tensor") == 0
+    pieces = jnp.stack([block] + [exchange(block, 4 * d, 4 * d) for d in (1, 2, 3)])
+    own = jnp.stack([pick(pieces, outer ^ d) for d in range(4)])
+    turned = exchange(own, 2, 1)
+    both = exchange(jnp.stack([own, turned]), 1, 2)
+    flip_one = jnp.where(first, both[0], turned)
+    flip_two = jnp.where(first, turned, both[0])
+    groups = jnp.stack([own, flip_one, flip_two, both[1]])
+    placed = jnp.stack([pick(groups, inner ^ j) for j in range(4)], axis=1)
+    return placed.reshape(16 * rows, columns)
+
+
+def scatter_sum(whole):
+    count = lax.axis_size("dp")
+    if count != 16:
+        return lax.psum_scatter(whole, "dp", scatter_dimension=0, tiled=True)
+    rows, columns = whole.shape[0] // count, whole.shape[1]
+    place = lax.axis_index("dp")
+    inner, outer = place % 4, place // 4
+    first = lax.axis_index("tensor") == 0
+    near = jnp.where(first, 2, 1)
+    groups = whole.reshape(4, 4, rows, columns)
+
+    def group(flip):
+        return lax.dynamic_index_in_dim(groups, inner ^ flip, 1, keepdims=False)
+
+    sent = exchange(jnp.stack([group(near), group(3)]).astype(BF), 2, 1).astype(F32)
+    sent_two = exchange((group(3 - near) + sent[1]).astype(BF), 1, 2).astype(F32)
+    plane = group(0) + sent[0] + sent_two
+    total = pick(plane, outer)
+    arrived = [exchange(pick(plane, outer ^ d).astype(BF), 4 * d, 4 * d) for d in (1, 2, 3)]
+    for part in arrived:
+        total = total + part.astype(F32)
+    return total
+
+
+def sum_everywhere(block):
+    count = lax.axis_size("dp")
+    if count & (count - 1):
+        return lax.psum(block, "dp")
+    flip = 1
+    while flip < count:
+        block = block + exchange(block, flip, flip)
+        flip *= 2
+    return block
+
+
+def eye_block(first_row, rows, columns):
+    row = lax.broadcasted_iota(jnp.int32, (rows, columns), 0) + first_row
+    return row == lax.broadcasted_iota(jnp.int32, (rows, columns), 1)
+
+
+def nn(left, right):
+    return lax.dot_general(left, right, (((1,), (0,)), ((), ())), preferred_element_type=F32)
+
+
+def nt(left, right):
+    return lax.dot_general(left, right, (((1,), (1,)), ((), ())), preferred_element_type=F32)
+
+
+def ns_kernel(x_ref, o_ref, y_ref, a_ref, ab_ref, p_ref, pb_ref, r_ref, rb_ref, col_ref, row_ref):
+    blk = 256
+    steps = D // blk
+    columns = x_ref.shape[1]
+    chunk = 768
+
+    def put(full_ref, half_ref, slot, i, value):
+        rows = pl.ds(pl.multiple_of(i * blk, blk), blk)
+        eye = eye_block(i * blk, blk, D)
+        only = jnp.where(eye, value, 0.0)
+        full_ref[rows, :] = value
+        half_ref[rows, :] = jnp.where(eye, 0.0, value).astype(BF)
+        col_ref[slot, rows, :] = jnp.sum(only, axis=1, keepdims=True)
+        part = jnp.sum(only, axis=0, keepdims=True)
+
+        @pl.when(i == 0)
+        def _():
+            row_ref[slot] = part
+
+        @pl.when(i > 0)
+        def _():
+            row_ref[slot] = row_ref[slot] + part
+
+    def gram(src):
+        def outer(i, carry):
+            rows = pl.ds(pl.multiple_of(i * blk, blk), blk)
+
+            def inner(k, carry):
+                cols = pl.ds(pl.multiple_of(k * chunk, chunk), chunk)
+                part = nt(src[rows, cols], src[:, cols])
+
+                @pl.when(k == 0)
+                def _():
+                    r_ref[rows, :] = part
+
+                @pl.when(k > 0)
+                def _():
+                    r_ref[rows, :] = r_ref[rows, :] + part
+
+                return carry
+
+            return lax.fori_loop(0, columns // chunk, inner, carry)
+
+        lax.fori_loop(0, steps, outer, 0)
+
+    def keep_gram(scale):
+        def step(i, carry):
+            rows = pl.ds(pl.multiple_of(i * blk, blk), blk)
+            put(a_ref, ab_ref, 0, i, r_ref[rows, :] * scale)
+            return carry
+
+        lax.fori_loop(0, steps, step, 0)
+
+    def polynomial(turn):
+        def step(i, carry):
+            rows = pl.ds(pl.multiple_of(i * blk, blk), blk)
+            eye = eye_block(i * blk, blk, D)
+            dcol, drow = col_ref[0, rows, :], row_ref[0]
+            square = nn(ab_ref[rows, :], ab_ref[...])
+            value = NS_C * square + a_ref[rows, :] * (NS_B + NS_C * (dcol + drow))
+            value = value + jnp.where(eye, NS_A - NS_C * dcol * dcol, 0.0)
+            put(p_ref, pb_ref.at[turn], 2 + turn, i, value)
+            return carry
+
+        lax.fori_loop(0, steps, step, 0)
+
+    def times(left, left_half, lslot, right, right_half, rslot, out, out_half, oslot):
+        def step(i, carry):
+            rows = pl.ds(pl.multiple_of(i * blk, blk), blk)
+            eye = eye_block(i * blk, blk, D)
+            lcol, rrow = col_ref[lslot, rows, :], row_ref[rslot]
+            value = nn(left_half[rows, :], right_half[...])
+            value = value + lcol * right[rows, :] + left[rows, :] * rrow
+            value = value - jnp.where(eye, lcol * rrow, 0.0)
+            put(out, out_half, oslot, i, value)
+            return carry
+
+        lax.fori_loop(0, steps, step, 0)
+
+    gram(x_ref)
+
+    def trace_step(i, total):
+        rows = pl.ds(pl.multiple_of(i * blk, blk), blk)
+        return total + jnp.sum(jnp.where(eye_block(i * blk, blk, D), r_ref[rows, :], 0.0))
+
+    trace = lax.fori_loop(0, steps, trace_step, jnp.float32(0.0))
+    root = jnp.sqrt(jnp.full((1, 1), trace, F32)) + 1e-07
+    keep_gram(1.0 / (root * root))
+    polynomial(0)
+    inverse = 1.0 / root
+
+    def apply_outer(i, carry):
+        rows = pl.ds(pl.multiple_of(i * blk, blk), blk)
+
+        def apply_inner(k, carry):
+            cols = pl.ds(pl.multiple_of(k * chunk, chunk), chunk)
+            value = nn(pb_ref[0, rows, :], x_ref[:, cols])
+            value = value + col_ref[2, rows, :] * x_ref[rows, cols].astype(F32)
+            y_ref[rows, cols] = (value * inverse).astype(BF)
+            return carry
+
+        return lax.fori_loop(0, columns // chunk, apply_inner, carry)
+
+    lax.fori_loop(0, steps, apply_outer, 0)
+    gram(y_ref)
+    keep_gram(1.0)
+
+    def turn_body(turn, carry):
+        polynomial(turn)
+        times(p_ref, pb_ref.at[turn], 2 + turn, a_ref, ab_ref, 0, r_ref, rb_ref, 1)
+        times(r_ref, rb_ref, 1, p_ref, pb_ref.at[turn], 2 + turn, a_ref, ab_ref, 0)
+        return carry
+
+    lax.fori_loop(1, NS_ITERS - 1, turn_body, 0)
+    polynomial(NS_ITERS - 1)
+
+    wanted = o_ref.shape[0]
+    eye = eye_block(0, wanted, D)
+    r_ref[:wanted, :] = p_ref[:wanted, :]
+
+    def chain(step, carry):
+        turn = NS_ITERS - 2 - step
+        left = r_ref[:wanted, :]
+        only = jnp.where(eye, left, 0.0)
+        lcol = jnp.sum(only, axis=1, keepdims=True)
+        off = left - only
+        right_half = pb_ref[turn]
+        drow = row_ref[2 + turn]
+        value = nn(off.astype(BF), right_half)
+        value = value + lcol * right_half[:wanted, :].astype(F32) + left * drow
+        r_ref[:wanted, :] = value
+        return carry
+
+    lax.fori_loop(0, NS_ITERS - 2, chain, 0)
+    left = r_ref[:wanted, :]
+    only = jnp.where(eye, left, 0.0)
+    lcol = jnp.sum(only, axis=1, keepdims=True)
+    off = (left - only).astype(BF)
+    kept = o_ref.shape[1]
+    for k in range(kept // chunk):
+        cols = slice(k * chunk, (k + 1) * chunk)
+        value = nn(off, y_ref[:, cols]) + lcol * y_ref[:wanted, cols].astype(F32)
+        o_ref[:, cols] = value.astype(BF)
+
+
+def orthogonal_rows(matrix, wanted, kept):
+    vmem = pl.BlockSpec(memory_space=pltpu.VMEM)
+    return pl.pallas_call(
+        ns_kernel,
+        out_shape=jax.ShapeDtypeStruct((wanted, kept), BF),
+        in_specs=[vmem],
+        out_specs=vmem,
+        scratch_shapes=[
+            pltpu.VMEM(matrix.shape, BF),
+            pltpu.VMEM((D, D), F32),
+            pltpu.VMEM((D, D), BF),
+            pltpu.VMEM((D, D), F32),
+            pltpu.VMEM((NS_ITERS, D, D), BF),
+            pltpu.VMEM((D, D), F32),
+            pltpu.VMEM((D, D), BF),
+            pltpu.VMEM((2 + NS_ITERS, D, 1), F32),
+            pltpu.VMEM((2 + NS_ITERS, 1, D), F32),
+        ],
+        compiler_params=pltpu.CompilerParams(vmem_limit_bytes=60 * 1024 * 1024),
+        cost_estimate=pl.CostEstimate(flops=30 * D**3 * 2, bytes_accessed=2 * matrix.size, transcendentals=0),
+        name="newton_schulz",
+    )(matrix)
+
+
+def own_matrix(packed, starts, widths):
+    place = lax.axis_index("dp")
+    rows = packed.shape[0]
+    widest = max(widths)
+    start = jnp.array(starts, jnp.int32)
+    width = jnp.array(widths, jnp.int32)
+    spare = max(0, starts[-1] + widest - packed.shape[1], max(starts) + widest - packed.shape[1])
+    packed = jnp.pad(packed, ((0, 0), (0, spare)))
+    inner = place % 4
+
+    def columns_of(whole, which):
+        return lax.dynamic_slice_in_dim(whole, pick(start, which), widest, whole.ndim - 1)
+
+    if lax.axis_size("dp") == 16:
+        planes = jnp.stack([packed] + [exchange(packed, 4 * d, 4 * d) for d in (1, 2, 3)])
+        mine = [columns_of(planes, inner)]
+        for d in (1, 2, 3):
+            mine.append(exchange(columns_of(planes, inner ^ d), d, d))
+        whole = jnp.stack(mine, axis=1).reshape(16 * rows, widest)
+    else:
+        whole = lax.all_gather(packed, "dp", axis=0, tiled=True)
+        whole = columns_of(whole, inner)
+        count = lax.axis_size("dp")
+        turn = (jnp.arange(count) + place // 4 * 4) % count
+        turn = jnp.concatenate([turn[:4][jnp.arange(4) ^ inner], turn[4:]])
+        whole = whole.reshape(count, rows, widest)[turn].reshape(count * rows, widest)
+    whole = jnp.where(jnp.arange(widest) < pick(width, inner), whole, jnp.zeros_like(whole))
+    return jnp.concatenate([whole, swap_cores(whole)], axis=1)
+
+
+def rows_of_all(block, rows):
+    inner = lax.axis_index("dp") % 4
+    parts = [block[:rows]]
+    for d in (1, 2, 3):
+        parts.append(exchange(block[d * rows : (d + 1) * rows], d, d))
+    parts = jnp.stack(parts)
+    return [pick(parts, inner ^ j).astype(F32) for j in range(4)]
 
 
 def layer_norm(values_in, gain_row, shift_row):
@@ -46,10 +332,6 @@
 
 def dense(left_in, right_in):
     return jnp.dot(left_in, right_in, preferred_element_type=jnp.float32)
-
-
-def dense_exact(left_in, right_in):
-    return jnp.dot(left_in, right_in, precision=HIGHEST)
 
 
 def dense_tn(left_in, right_in):
@@ -124,48 +406,6 @@
     return (jnp.concatenate(grad_query_parts, 0), grad_keys, grad_values)
 
 
-def gram_branch(width):
-
-    def gram_compute(iterate):
-        part_cols = iterate[:, :width]
-        return lax.dot_general(part_cols, part_cols, (((1,), (1,)), ((), ())), precision=HIGHEST)
-
-    return gram_compute
-
-
-def apply_branch(width, columns):
-
-    def apply_compute(poly_term, iterate):
-        product = dense_exact(poly_term, iterate[:, :width])
-        return jnp.pad(product, ((0, 0), (0, columns - width)))
-
-    return apply_compute
-
-
-def newton_schulz(matrix, which, widths):
-    columns = matrix.shape[1]
-    gram_fns = [gram_branch(width) for width in widths]
-    apply_fns = [apply_branch(width, columns) for width in widths]
-    iterate = matrix
-    for turn in range(NS_ITERS):
-        gram_matrix = jax.tree.map(
-            lambda part: part.astype(jnp.float32),
-            lax.psum(for_sending(lax.switch(which, gram_fns, iterate)), "tensor"),
-        )
-        if turn == 0:
-            root = jnp.sqrt(jnp.trace(gram_matrix)) + 1e-07
-            gram_matrix = gram_matrix / (root * root)
-        poly_term = NS_B * gram_matrix + NS_C * dense_exact(gram_matrix, gram_matrix)
-        iterate = NS_A * iterate + lax.switch(which, apply_fns, poly_term, iterate)
-        if turn == 0:
-            iterate = iterate / root
-    return iterate
-
-
-def widen(matrix, columns):
-    return jnp.pad(matrix, ((0, 0), (0, columns - matrix.shape[1])))
-
-
 def body(
     tokens,
     cotangent,
@@ -193,7 +433,6 @@
     mom_hidden_bias,
 ):
     dp_count = lax.axis_size("dp")
-    tensor_count = lax.axis_size("tensor")
     seq_count, length, model_width = tokens.shape
     row_count = seq_count * length
     shard_rows = w_qkv.shape[0]
@@ -201,13 +440,14 @@
     hidden_part = w_up.shape[1]
     heads_part = half_width // DH
     widths = [3 * half_width, half_width, hidden_part, hidden_part]
-    full_qkv, full_out, full_up, full_down = (
-        lax.all_gather(w_qkv.astype(jnp.bfloat16), "dp", axis=0, tiled=True),
-        lax.all_gather(w_out.astype(jnp.bfloat16), "dp", axis=1, tiled=True),
-        lax.all_gather(w_up.astype(jnp.bfloat16), "dp", axis=0, tiled=True),
-        lax.all_gather(w_down.astype(jnp.bfloat16), "dp", axis=1, tiled=True),
-    )
-    qkv_matrix = full_qkv.reshape(model_width, 3 * half_width)
+    starts = [0, widths[0], widths[0] + widths[1], widths[0] + widths[1] + widths[2]]
+    low_weights = jnp.concatenate(
+        [w_qkv.reshape(shard_rows, 3 * half_width), w_out.T, w_up, w_down.T], axis=1
+    ).astype(BF)
+    first_weights = gather_rows(low_weights[:, : starts[2]])
+    last_weights = lax.all_gather(low_weights[:, starts[2] :], "dp", axis=0, tiled=True)
+    qkv_matrix, out_rows = first_weights[:, : starts[1]], first_weights[:, starts[1] :]
+    full_up, down_rows = last_weights[:, :hidden_part], last_weights[:, hidden_part:]
     flat_in = tokens.reshape(row_count, model_width).astype(jnp.float32)
     normed_f, norm_one_pull = jax.vjp(layer_norm, flat_in, norm_gains[0], row_biases[0])
     normed_one = normed_f.astype(jnp.bfloat16)
@@ -222,30 +462,31 @@
     values_low = raw_qkv[:, 2].astype(jnp.bfloat16).reshape(seq_shape)
     mixed_f, totals = lax.map(attend_forward, (query_low, keys_low, values_low, image_ids))
     mixed_heads = mixed_f.reshape(row_count, half_width).astype(jnp.bfloat16)
-    attn_out = lax.psum(dense(mixed_heads, full_out), "tensor") + row_biases[1]
+    attn_part = dense_nt(mixed_heads, out_rows).astype(BF)
+    attn_out = attn_part.astype(F32) + swap_cores(attn_part).astype(F32) + row_biases[1]
     residual = flat_in + attn_out
     normed_two_f, norm_two_pull = jax.vjp(layer_norm, residual, norm_gains[1], row_biases[2])
     normed_two = normed_two_f.astype(jnp.bfloat16)
     pre_act = dense(normed_two, full_up) + hidden_bias
     act_f, gelu_pull = jax.vjp(gelu_tanh, pre_act)
     act_out = act_f.astype(jnp.bfloat16)
-    mlp_out = (
-        lax.psum(dense(act_out, full_down).astype(jnp.bfloat16), "tensor").astype(jnp.float32)
-        + row_biases[3]
-    )
+    mlp_part = dense_nt(act_out, down_rows).astype(BF)
+    mlp_out = mlp_part.astype(F32) + swap_cores(mlp_part).astype(F32) + row_biases[3]
     block_out = (residual + mlp_out).reshape(tokens.shape)
     grad_y = cotangent.reshape(row_count, model_width).astype(jnp.float32)
     grad_y_low = grad_y.astype(jnp.bfloat16)
-    grad_down_local = dense_tn(act_out, grad_y_low)
-    (grad_pre,) = gelu_pull(dense_nt(grad_y_low, full_down))
+    grad_down_local = dense_tn(grad_y_low, act_out)
+    (grad_pre,) = gelu_pull(dense(grad_y_low, down_rows))
     grad_pre_low = grad_pre.astype(jnp.bfloat16)
     grad_up_local = dense_tn(normed_two, grad_pre_low)
-    grad_normed_two = lax.psum(dense_nt(grad_pre_low, full_up), "tensor")
+    part_two = dense_nt(grad_pre_low, full_up).astype(BF)
+    grad_normed_two = part_two.astype(F32) + swap_cores(part_two).astype(F32)
+    late = scatter_sum(jnp.concatenate([grad_up_local, grad_down_local], axis=1))
     grad_resid_ln, grad_gain_two, grad_shift_two = norm_two_pull(grad_normed_two)
     grad_resid = grad_y + grad_resid_ln
     grad_resid_low = grad_resid.astype(jnp.bfloat16)
-    grad_out_local = dense_tn(mixed_heads, grad_resid_low)
-    grad_mixed = dense_nt(grad_resid_low, full_out).astype(jnp.bfloat16).reshape(seq_shape)
+    grad_out_local = dense_tn(grad_resid_low, mixed_heads)
+    grad_mixed = dense(grad_resid_low, out_rows).astype(jnp.bfloat16).reshape(seq_shape)
     grad_query, grad_keys, grad_values = lax.map(
         attend_backward, (query_low, keys_low, values_low, image_ids, totals, grad_mixed)
     )
@@ -258,75 +499,49 @@
     ).reshape(row_count, 3 * half_width)
     grad_qkv_bias_local = jnp.sum(grad_raw, axis=0).reshape(3, half_width)
     grad_raw_low = grad_raw.astype(jnp.bfloat16)
-    grad_qkv_local = dense_tn(normed_one, grad_raw_low).reshape(model_width, 3, half_width)
-    grad_normed_one = lax.psum(
-        dense_nt(grad_raw_low, qkv_matrix).astype(jnp.bfloat16), "tensor"
-    ).astype(jnp.float32)
+    grad_qkv_local = dense_tn(normed_one, grad_raw_low)
+    early = scatter_sum(jnp.concatenate([grad_qkv_local, grad_out_local], axis=1))
+    part_one = dense_nt(grad_raw_low, qkv_matrix).astype(BF)
+    grad_normed_one = part_one.astype(F32) + swap_cores(part_one).astype(F32)
     grad_flat_ln, grad_gain_one, grad_shift_one = norm_one_pull(grad_normed_one)
     tokens_grad = (grad_resid + grad_flat_ln).reshape(tokens.shape)
-    grad_qkv, grad_out, grad_up, grad_down = (
-        lax.psum_scatter(grad_qkv_local, "dp", scatter_dimension=0, tiled=True),
-        lax.psum_scatter(grad_out_local, "dp", scatter_dimension=1, tiled=True),
-        lax.psum_scatter(grad_up_local, "dp", scatter_dimension=0, tiled=True),
-        lax.psum_scatter(grad_down_local, "dp", scatter_dimension=1, tiled=True),
-    )
-    own_mask = (jnp.arange(tensor_count) == lax.axis_index("tensor")).astype(jnp.float32)
-    gains_local = 0.5 * jnp.stack([grad_gain_one, grad_gain_two])
-    biases_local = 0.5 * jnp.stack(
-        [grad_shift_one, jnp.sum(grad_resid, axis=0), grad_shift_two, jnp.sum(grad_y, axis=0)]
-    )
-    qkv_bias_spread = own_mask[None, :, None] * grad_qkv_bias_local[:, None, :]
-    hidden_spread = own_mask[:, None] * jnp.sum(grad_pre, axis=0)[None, :]
-    summed = lax.psum(
-        (
-            gains_local,
-            biases_local,
-            grad_head_local,
-            grad_qshift_local,
-            qkv_bias_spread,
-            hidden_spread,
-        ),
-        ("dp", "tensor"),
-    )
-    grad_gains = summed[0]
-    grad_biases = summed[1]
-    grad_head_gains = summed[2]
-    grad_query_bias = summed[3]
-    grad_qkv_bias = jnp.sum(summed[4] * own_mask[None, :, None], axis=1)
-    grad_hidden_bias = jnp.sum(summed[5] * own_mask[:, None], axis=0)
+    grad_rows = [early[:, : starts[1]], early[:, starts[1] :], late[:, :hidden_part], late[:, hidden_part:]]
+    grad_qkv = grad_rows[0].reshape(shard_rows, 3, half_width)
+    grad_out, grad_up, grad_down = grad_rows[1].T, grad_rows[2], grad_rows[3].T
     next_mom_qkv = 0.5 * mom_qkv + grad_qkv
     next_mom_out = 0.5 * mom_out + grad_out
     next_mom_up = 0.5 * mom_up + grad_up
     next_mom_down = 0.5 * mom_down + grad_down
-    row_mats = (
-        next_mom_qkv.reshape(shard_rows, 3 * half_width),
-        next_mom_out.T,
-        next_mom_up,
-        next_mom_down.T,
-    )
-    dp_index = lax.axis_index("dp")
-    owned = dp_index % 4
-    gathered = (
-        lax.all_gather(row_mats[0].astype(jnp.bfloat16), "dp", axis=0, tiled=True).astype(
-            jnp.float32
-        ),
-        lax.all_gather(row_mats[1].astype(jnp.bfloat16), "dp", axis=0, tiled=True).astype(
-            jnp.float32
-        ),
-        lax.all_gather(row_mats[2].astype(jnp.bfloat16), "dp", axis=0, tiled=True).astype(
-            jnp.float32
-        ),
-        lax.all_gather(row_mats[3].astype(jnp.bfloat16), "dp", axis=0, tiled=True).astype(
-            jnp.float32
-        ),
-    )
-    all_moments = jnp.stack([widen(whole, hidden_part) for whole in gathered])
-    own_matrix = lax.dynamic_index_in_dim(all_moments, owned, 0, keepdims=False)
-    orthogonal = newton_schulz(own_matrix, owned, widths)
-    own_rows = []
-    for owner in range(4):
-        full_result = from_root(for_sending(orthogonal[:, : widths[owner]]), "dp", owner)
-        own_rows.append(lax.dynamic_slice_in_dim(full_result, dp_index * shard_rows, shard_rows, 0))
+    packed = jnp.concatenate(
+        [next_mom_qkv.reshape(shard_rows, 3 * half_width), next_mom_out.T, next_mom_up, next_mom_down.T],
+        axis=1,
+    ).astype(BF)
+    matrix = own_matrix(packed, starts, widths)
+    own_rows = rows_of_all(orthogonal_rows(matrix, 4 * shard_rows, hidden_part), shard_rows)
+    small = [
+        jnp.stack([grad_gain_one, grad_gain_two]),
+        jnp.stack([grad_shift_one, jnp.sum(grad_resid, axis=0), grad_shift_two, jnp.sum(grad_y, axis=0)]),
+        grad_qkv_bias_local,
+        jnp.sum(grad_pre, axis=0),
+        grad_head_local,
+        grad_qshift_local,
+    ]
+    sizes = [part.size for part in small]
+    flat = jnp.concatenate([part.reshape(-1) for part in small])
+    flat = jnp.pad(flat, (0, -flat.size % 1024)).reshape(-1, 128)
+    summed = sum_everywhere(flat)
+    cut = sum(sizes[:4])
+    summed = summed.reshape(-1)
+    heads = summed[cut : cut + sizes[4] + sizes[5]]
+    heads = heads + swap_cores(heads)
+    pieces = []
+    at = 0
+    for part, size in zip(small[:4], sizes):
+        pieces.append(summed[at : at + size].reshape(part.shape))
+        at += size
+    grad_gains, grad_biases, grad_qkv_bias, grad_hidden_bias = pieces
+    grad_head_gains = heads[: sizes[4]].reshape(grad_head_local.shape)
+    grad_query_bias = heads[sizes[4] :]
     rate_muon = step_rates[0]
     new_w_qkv = w_qkv - rate_muon * (0.2 * math.sqrt(max(D, 3 * D))) * own_rows[0][
         :, : 3 * half_width

time: 1800 us -> 513 us (0.28)
  waiting for transfers between devices: 1090 us -> 132 us
  matrix products: 248 us -> 97.1 us
  blocking collectives: 133 us -> 0 us
  loops' own time: 96.5 us -> 0 us
  Pallas kernels: 0 us -> 53.2 us
  local copies, waits for them, and re-layouts: 61.2 us -> 42.1 us
    reduce_scatter x4 -> x0, waiting for transfers between devices: 521 us -> none  [the longest x1 141 us: body(): lax.psum_scatter(grad_up_local, 'dp', scatter_dimension=0, tiled=True)]
    psum x8 -> x0, waiting for transfers between devices: 293 us -> none  [the longest x1 160 us: from_root(): return lax.psum(block, axis)]
    all_gather x6 -> x1, waiting for transfers between devices: 273 us -> 0.02 us  [body(): lax.all_gather(low_weights[:, starts[2]:], 'dp', axis=0, tiled=True)]
    ppermute x0 -> x34, waiting for transfers between devices: none -> 132 us  [the longest x28 132 us: exchange(): return lax.ppermute(block, BOTH, pairs)]
    dot_general x15 -> x0, matrix products: 131 us -> none  [the longest x10 76.7 us: dense_exact(): return jnp.dot(left_in, right_in, precision=HIGHEST)]
    another operation x10 -> x0, loops' own time: 96.5 us -> none  [the longest x5 64.5 us: newton_schulz(): lax.switch(which, gram_fns, iterate)]
    all_gather x2 -> x0, blocking collectives: 90.1 us -> none  [the longest x1 46.6 us: body(): lax.all_gather(w_out.astype(jnp.bfloat16), 'dp', axis=1, tiled=True)]
    pallas_call x0 -> x1, Pallas kernels: none -> 53.2 us  [orthogonal_rows(): pl.pallas_call(ns_kernel, out_shape=jax.ShapeDtypeStruct((wanted, kept),...]
  transfers between devices with their start and end apart: 18 -> 35, of which waited for: 18 -> 18; matrix products, arithmetic and copies ran while one was open for 5% -> 41% of each run, Pallas kernels for 0% -> 0%
where the time goes in v1:
time: 513 us; the launch traced here: 504 us
  waiting for transfers between devices  132 us (26%)
  other arithmetic  117 us (23%)
  matrix products  97.1 us (19%)
  Pallas kernels  53.2 us (10%)
  local copies, waits for them, and re-layouts  42.1 us (8%)
  starting transfers between devices  36.1 us (7%)
  between operations  26.9 us (5%)
    ppermute x28, waiting for transfers between devices, exchange(): return lax.ppermute(block, BOTH, pairs)  132 us
    pallas_call x1, Pallas kernels, orthogonal_rows(): pl.pallas_call(ns_kernel, out_shape=jax.ShapeDtypeStruct((wanted, kept),...  53.2 us
    ppermute x28, starting transfers between devices, exchange(): return lax.ppermute(block, BOTH, pairs)  35.4 us
    unnamed x252, local copies, waits for them, and re-layouts  21.9 us
    dot_general x4, matrix products, dense(): return jnp.dot(left_in, right_in, preferred_element_type=jnp.float32)  19.7 us
    convert_element_type x2, other arithmetic, attend_backward(): grad_scores = grad_scores.astype(jnp.bfloat16)  18.4 us
    dot_general x4, matrix products, dense_tn(): lax.dot_general(left_in, right_in, (((0,), (0,)), ((), ())), preferred_el...  14 us
    dot_general x2, matrix products, attend_backward(): jnp.einsum('qhd,khd->hqk', grad_rows, values, preferred_element_type=jnp....  13.6 us
  transfers between devices with their start and end apart: 35, of which 18 were waited for; matrix products, arithmetic and copies ran while one was open for 41% of the time, Pallas kernels for 0%

profile of v1, /device:TPU:0, one launch (start us, length us, event | category | flops | bytes accessed | tf_op | source)
XLA Modules:
  0.0 504.1 jit_solution(16415102188757151390)
XLA Ops:
  16.9 5.1 %collective-permute-done.1 = bf16[48,1536]{1,0:T(8,128)(2,1)S(1)} collective-permute-done((bf16[48,1536]{1,0:T(8,128)(2,1)S(1)}, bf16[48,1536]{1,0:T(8,128)(2,1)S(1)}, u32[]{:S(2)}, u32[]{:S(2)}) %collective-permute-start.1) | collective-permute-done | bytes 147488 | tf_op jit(solution)/shard_map/ppermute | solution.py:31
  30.2 5.6 %collective-permute-done.3 = bf16[4,48,1536]{2,1,0:T(8,128)(2,1)S(1)} collective-permute-done((bf16[4,48,1536]{2,1,0:T(8,128)(2,1)}, bf16[4,48,1536]{2,1,0:T(8,128)(2,1)S(1)}, u32[]{:S(2)}, u32[]{:S(2)}) %collective-permute-start.3) | collective-permute-done | bytes 589856 | tf_op jit(solution)/shard_map/ppermute | solution.py:31
  39.3 15.1 %collective-permute-done.4 = bf16[2,4,48,1536]{3,2,1,0:T(8,128)(2,1)S(1)} collective-permute-done((bf16[2,4,48,1536]{3,2,1,0:T(8,128)(2,1)S(1)}, bf16[2,4,48,1536]{3,2,1,0:T(8,128)(2,1)S(1)}, u32[]{:S(2)}, u32[]{:S(2)}) %collective-permute-start.4) | collective-permute-done | bytes 1179680 | tf_op jit(solution)/shard_map/ppermute | solution.py:31
  62.4 6.1 %copy.79 = f32[1024,1152]{0,1:T(8,128)} copy(f32[1024,1152]{1,0:T(8,128)} %convolution_add_fusion) | data formatting | bytes 9437184 | tf_op jit(solution)/shard_map/add | solution.py:454
  90.8 7.5 %fusion.72 = bf16[512,6,64]{0,2,1:T(8,128)(2,1)S(1)} fusion(f32[6,512,1024]{2,1,0:T(8,128)} %copy-done.1, f32[6,512]{1,0:T(8,128)S(1)} %log_add_fusion.1, pred[512,1024]{1,0:T(8,128)(4,1)S(1)} %get-tuple-element.241, f32[1024,3,6,64]{0,3,2,1:T(8,128)S(1)} %bitcast.367), kind=kOutput, calls=%fused_computation.140 | convolution fusion | flops 412286976 | bytes 14303232 | tf_op jit(solution)/shard_map/while/body/eval_jaxpr/hqk,khd->qhd/dot_general | solution.py:369
  110.1 5.7 %fusion.41 = f32[1024,1536]{1,0:T(8,128)S(1)} fusion(bf16[768,3072]{1,0:T(8,128)(2,1)} %all-gather.2.cloned.1.call-done, f32[1024,768]{0,1:T(8,128)} %copy-done.5, f32[768]{0:T(1024)S(1)} %get-tuple-element.166, f32[768]{0:T(1024)S(1)} %get-tuple-element.266, f32[1024]{0:T(1024)S(1)} %fusion.114, f32[1024]{0:T(1024)S(1)} %broadcast_multiply_fusion.2), kind=kOutput, calls=%fused_computation.89 | convolution fusion | flops 2419851264 | bytes 11810816 | tf_op jit(solution)/shard_map/dot_general | solution.py:334
  120.6 7.3 %fusion.133 = (f32[1536]{0:T(1024)}, bf16[1024,1536]{1,0:T(8,128)(2,1)S(1)}) fusion(f32[1024,1536]{1,0:T(8,128)S(1)} %fusion.41, f32[1536]{0:T(1024)S(1)} %copy-done.87, bf16[768,3072]{1,0:T(8,128)(2,1)S(1)} %bitcast.424, bf16[1,1024,768]{2,1,0:T(8,128)(2,1)S(1)} %copy-done.33), kind=kOutput, calls=%fused_computation.307 | convolution fusion | flops 2450520576 | bytes 13383680 | tf_op jit(solution)/shard_map/dot_general | solution.py:334
  139.9 8.4 %pad_maximum_fusion = f32[768,3072]{1,0:T(8,128)} fusion(f32[768,1536]{1,0:T(8,128)} %convolution_bitcast_fusion, f32[768,1536]{1,0:T(8,128)} %fusion.63), kind=kLoop, calls=%fused_computation.10 | loop fusion | flops 2359296 | bytes 18874368 | tf_op jit(solution)/shard_map/concatenate | solution.py:484
  171.6 6.9 %multiply_reduce_fusion.1 = (f32[6,512]{1,0:T(8,128)S(1)}, f32[6,512,1024]{2,1,0:T(8,128)}) fusion(f32[6,512,1024]{2,1,0:T(8,128)S(1)} %bitcast.362, f32[6,512]{1,0:T(8,128)S(1)} %log_add_fusion.1, pred[512,1024]{1,0:T(8,128)(4,1)S(1)} %get-tuple-element.241, bf16[512,6,64]{0,2,1:T(8,128)(2,1)S(1)} %bitcast.393, f32[1024,3,6,64]{0,3,2,1:T(8,128)S(1)} %bitcast.370), kind=kOutput, calls=%fused_computation.3 | convolution fusion | flops 415233024 | bytes 26898432 | tf_op jit(solution)/shard_map/while/body/eval_jaxpr/qhd,khd->hqk/dot_general | solution.py:387
  178.5 11.0 %multiply_convert_fusion.1 = bf16[6,512,1024]{2,1,0:T(8,128)(2,1)} fusion(f32[6,512,1024]{2,1,0:T(8,128)} %get-tuple-element.260, f32[6,512,1024]{2,1,0:T(8,128)S(1)} %bitcast.362, f32[6,512]{1,0:T(8,128)S(1)} %get-tuple-element.259, f32[6,512]{1,0:T(8,128)S(1)} %log_add_fusion.1, pred[512,1024]{1,0:T(8,128)(4,1)} %copy-done.14), kind=kLoop, calls=%fused_computation.2 | loop fusion | flops 15728640 | bytes 32006144 | tf_op jit(solution)/shard_map/while/body/eval_jaxpr/convert_element_type | solution.py:393
  189.5 5.9 %fusion.138 = f32[6,64,512]{2,1,0:T(8,128)} fusion(bf16[1024,6,64]{0,2,1:T(8,128)(2,1)S(1)} %copy-done.10, bf16[6,512,1024]{2,1,0:T(8,128)(2,1)} %multiply_convert_fusion.1), kind=kOutput, calls=%fused_computation.308 | convolution fusion | flops 402653184 | bytes 7864320 | tf_op jit(solution)/shard_map/while/body/eval_jaxpr/hqk,khd->qhd/dot_general | solution.py:395
  195.4 5.2 %fusion.97 = f32[6,64,1024]{2,1,0:T(8,128)} fusion(bf16[6,512,1024]{2,1,0:T(8,128)(2,1)} %multiply_convert_fusion.1, bf16[1024,6,64]{0,2,1:T(8,128)(2,1)S(1)} %copy-done.26), kind=kOutput, calls=%fused_computation.186 | convolution fusion | flops 402653184 | bytes 8257536 | tf_op jit(solution)/shard_map/while/body/eval_jaxpr/hqk,qhd->khd/dot_general | solution.py:397
  200.7 6.8 %multiply_reduce_fusion = (f32[6,512]{1,0:T(8,128)S(1)}, f32[6,512,1024]{2,1,0:T(8,128)}) fusion(f32[6,512,1024]{2,1,0:T(8,128)S(1)} %bitcast.360, f32[6,512]{1,0:T(8,128)S(1)} %log_add_fusion, pred[512,1024]{1,0:T(8,128)(4,1)S(1)} %copy-done.13, bf16[512,6,64]{0,2,1:T(8,128)(2,1)S(1)} %bitcast.390, f32[1024,3,6,64]{0,3,2,1:T(8,128)S(1)} %bitcast.371), kind=kOutput, calls=%fused_computation.1 | convolution fusion | flops 415233024 | bytes 26898432 | tf_op jit(solution)/shard_map/while/body/eval_jaxpr/qhd,khd->hqk/dot_general | solution.py:387
  210.4 7.4 %multiply_convert_fusion = bf16[6,512,1024]{2,1,0:T(8,128)(2,1)S(1)} fusion(f32[6,512,1024]{2,1,0:T(8,128)} %get-tuple-element.258, f32[6,512,1024]{2,1,0:T(8,128)S(1)} %bitcast.360, f32[6,512]{1,0:T(8,128)S(1)} %get-tuple-element.257, f32[6,512]{1,0:T(8,128)S(1)} %log_add_fusion, pred[512,1024]{1,0:T(8,128)(4,1)S(1)} %copy-done.13), kind=kLoop, calls=%fused_computation | loop fusion | flops 15728640 | bytes 32006144 | tf_op jit(solution)/shard_map/while/body/eval_jaxpr/convert_element_type | solution.py:393
  270.2 11.6 %collective-permute-done.10 = bf16[4,48,1536]{2,1,0:T(8,128)(2,1)S(1)} collective-permute-done((bf16[4,48,1536]{2,1,0:T(8,128)(2,1)S(1)}, bf16[4,48,1536]{2,1,0:T(8,128)(2,1)S(1)}, u32[]{:S(2)}, u32[]{:S(2)}) %collective-permute-start.10) | collective-permute-done | bytes 589856 | tf_op jit(solution)/shard_map/ppermute | solution.py:31
  289.7 6.2 %collective-permute-done.13 = bf16[48,1536]{1,0:T(8,128)(2,1)S(1)} collective-permute-done((bf16[48,1536]{1,0:T(8,128)(2,1)S(1)}, bf16[48,1536]{1,0:T(8,128)(2,1)S(1)}, u32[]{:S(2)}, u32[]{:S(2)}) %collective-permute-start.13) | collective-permute-done | bytes 147488 | tf_op jit(solution)/shard_map/ppermute | solution.py:31
  308.6 9.5 %collective-permute-done.16 = bf16[48,3072]{1,0:T(8,128)(2,1)S(1)} collective-permute-done((bf16[48,3072]{1,0:T(8,128)(2,1)S(1)}, bf16[48,3072]{1,0:T(8,128)(2,1)S(1)}, u32[]{:S(2)}, u32[]{:S(2)}) %collective-permute-start.16) | collective-permute-done | bytes 294944 | tf_op jit(solution)/shard_map/ppermute | solution.py:31
  321.1 11.5 %collective-permute-done.17 = bf16[48,3072]{1,0:T(8,128)(2,1)S(1)} collective-permute-done((bf16[48,3072]{1,0:T(8,128)(2,1)S(1)}, bf16[48,3072]{1,0:T(8,128)(2,1)S(1)}, u32[]{:S(2)}, u32[]{:S(2)}) %collective-permute-start.17) | collective-permute-done | bytes 294944 | tf_op jit(solution)/shard_map/ppermute | solution.py:31
  339.8 10.7 %collective-permute-done.26 = bf16[48,4608]{1,0:T(8,128)(2,1)} collective-permute-done((bf16[48,4608]{1,0:T(8,128)(2,1)}, bf16[48,4608]{1,0:T(8,128)(2,1)}, u32[]{:S(2)}, u32[]{:S(2)}) %collective-permute-start.26) | collective-permute-done | bytes 442400 | tf_op jit(solution)/shard_map/ppermute | solution.py:31
  350.5 22.6 %collective-permute-done.25 = bf16[48,4608]{1,0:T(8,128)(2,1)} collective-permute-done((bf16[48,4608]{1,0:T(8,128)(2,1)}, bf16[48,4608]{1,0:T(8,128)(2,1)}, u32[]{:S(2)}, u32[]{:S(2)}) %collective-permute-start.25) | collective-permute-done | bytes 442400 | tf_op jit(solution)/shard_map/ppermute | solution.py:31
  386.7 15.0 %collective-permute-done.19 = f32[64,128]{1,0:T(8,128)S(1)} collective-permute-done((f32[64,128]{1,0:T(8,128)S(1)}, f32[64,128]{1,0:T(8,128)S(1)}, u32[]{:S(2)}, u32[]{:S(2)}) %collective-permute-start.19) | collective-permute-done | bytes 32800 | tf_op jit(solution)/shard_map/ppermute | solution.py:31
  411.1 5.4 %add_bitcast_fusion = f32[1,1024,768]{1,2,0:T(8,128)} fusion(f32[1024]{0:T(1024)S(1)} %negate_multiply_fusion.2, f32[1024,768]{0,1:T(8,128)S(1)} %copy-done.8, f32[1024]{0:T(1024)S(1)} %copy-done.69, bf16[1,1024,768]{1,2,0:T(8,128)(2,1)S(1)} %copy-done.23, f32[1024]{0:T(1024)S(1)} %copy-done.64, f32[1024]{0:T(1024)S(1)} %copy-done.54, ...), kind=kLoop, calls=%fused_computation.59 | loop fusion | flops 11796480 | bytes 12606464 | tf_op jit(solution)/shard_map/reshape | solution.py:507
  423.6 5.1 %pad_maximum_fusion.3.x_ref = bf16[768,3072]{1,0:T(8,128)(2,1)} fusion(bf16[768,1536]{1,0:T(8,128)(2,1)} %collective-permute-done.30, bf16[768,1536]{1,0:T(8,128)(2,1)} %bitcast_select_fusion), kind=kLoop, calls=%fused_computation.34 | loop fusion | flops 9437184 | bytes 9437184 | tf_op jit(solution)/shard_map/concatenate | solution.py:304
  428.7 53.2 %newton_schulz.1 = bf16[192,1536]{1,0:T(8,128)(2,1)} custom-call(bf16[768,3072]{1,0:T(8,128)(2,1)} %pad_maximum_fusion.3.x_ref), custom_call_target="tpu_custom_call" | custom-call | flops 27179089920 | bytes 4718592 | tf_op jit(solution)/shard_map/newton_schulz/pallas_call | solution.py:255
  (476 shorter events, 222.5 us)
Async XLA Ops:
  7.2 102.8 %all-gather.2.cloned.1.call-start = ((), (), s32[]{:S(2)}) async-start(), calls=%async_computation | async-start | bytes 5013504 | tf_op jit(solution)/shard_map/all_gather | solution.py:448
  9.2 12.8 %collective-permute-start.1 = (bf16[48,1536]{1,0:T(8,128)(2,1)S(1)}, bf16[48,1536]{1,0:T(8,128)(2,1)S(1)}, u32[]{:S(2)}, u32[]{:S(2)}) collective-permute-start(bf16[48,1536]{1,0:T(8,128)(2,1)S(1)} %get-tuple-element.240), channel_id=1, source_target_pairs={{0,16},{1,17},{2,18},{3,19},{4,20},{5,21},{6,22},{7,23},{8,24},{9,... | collective-permute-start | bytes 442376 | tf_op jit(solution)/shard_map/ppermute | solution.py:31
  25.7 10.1 %collective-permute-start.3 = (bf16[4,48,1536]{2,1,0:T(8,128)(2,1)}, bf16[4,48,1536]{2,1,0:T(8,128)(2,1)S(1)}, u32[]{:S(2)}, u32[]{:S(2)}) collective-permute-start(bf16[4,48,1536]{2,1,0:T(8,128)(2,1)} %get-tuple-element.234), channel_id=1, source_target_pairs={{0,4},{1,3},{2,6},{3,1},{4,0},{5,7},{6,2},{7,5},{8,12},{9,11},{10,... | collective-permute-start | bytes 1769480 | tf_op jit(solution)/shard_map/ppermute | solution.py:31
  36.0 18.4 %collective-permute-start.4 = (bf16[2,4,48,1536]{3,2,1,0:T(8,128)(2,1)S(1)}, bf16[2,4,48,1536]{3,2,1,0:T(8,128)(2,1)S(1)}, u32[]{:S(2)}, u32[]{:S(2)}) collective-permute-start(bf16[2,4,48,1536]{3,2,1,0:T(8,128)(2,1)S(1)} %pad_maximum_fusion.10), channel_id=1, source_target_pairs={{0,2},{1,5},{2,0},{3,7},{4,6},{5,1},{6,4},{7,3},{8,10},{9,13},{10,... | collective-permute-start | bytes 3538952 | tf_op jit(solution)/shard_map/ppermute | solution.py:31
  130.6 23.5 %collective-permute-start.7 = (bf16[1024,768]{0,1:T(8,128)(2,1)S(1)}, bf16[1024,768]{0,1:T(8,128)(2,1)S(1)}, u32[]{:S(2)}, u32[]{:S(2)}) collective-permute-start(bf16[1024,768]{0,1:T(8,128)(2,1)S(1)} %fusion.43), channel_id=1, source_target_pairs={{0,1},{1,0},{2,3},{3,2},{4,5},{5,4},{6,7},{7,6},{8,9},{9,8},{10,11... | collective-permute-start | bytes 4718600 | tf_op jit(solution)/shard_map/ppermute | solution.py:35
  139.6 16.7 %collective-permute-start.6 = (bf16[1024,768]{0,1:T(8,128)(2,1)}, bf16[1024,768]{0,1:T(8,128)(2,1)}, u32[]{:S(2)}, u32[]{:S(2)}) collective-permute-start(bf16[1024,768]{0,1:T(8,128)(2,1)} %fusion.46), channel_id=1, source_target_pairs={{0,1},{1,0},{2,3},{3,2},{4,5},{5,4},{6,7},{7,6},{8,9},{9,8},{10,11... | collective-permute-start | bytes 4718600 | tf_op jit(solution)/shard_map/ppermute | solution.py:35
  152.6 99.3 %collective-permute-start.14 = (bf16[2,4,48,3072]{3,2,1,0:T(8,128)(2,1)}, bf16[2,4,48,3072]{3,2,1,0:T(8,128)(2,1)}, u32[]{:S(2)}, u32[]{:S(2)}) collective-permute-start(bf16[2,4,48,3072]{3,2,1,0:T(8,128)(2,1)} %pad_maximum_fusion.6), channel_id=1, source_target_pairs={{0,4},{1,3},{2,6},{3,1},{4,0},{5,7},{6,2},{7,5},{8,12},{9,11},{10,... | collective-permute-start | bytes 7077896 | tf_op jit(solution)/shard_map/ppermute | solution.py:31
  231.7 28.9 %collective-permute-start.9 = (bf16[2,4,48,1536]{3,2,1,0:T(8,128)(2,1)}, bf16[2,4,48,1536]{3,2,1,0:T(8,128)(2,1)}, u32[]{:S(2)}, u32[]{:S(2)}) collective-permute-start(bf16[2,4,48,1536]{3,2,1,0:T(8,128)(2,1)} %pad_maximum_fusion.11), channel_id=1, source_target_pairs={{0,4},{1,3},{2,6},{3,1},{4,0},{5,7},{6,2},{7,5},{8,12},{9,11},{10,... | collective-permute-start | bytes 3538952 | tf_op jit(solution)/shard_map/ppermute | solution.py:31
  237.2 26.0 %collective-permute-start.8 = (bf16[1024,768]{0,1:T(8,128)(2,1)}, bf16[1024,768]{0,1:T(8,128)(2,1)}, u32[]{:S(2)}, u32[]{:S(2)}) collective-permute-start(bf16[1024,768]{0,1:T(8,128)(2,1)} %convolution_convert_fusion.1), channel_id=1, source_target_pairs={{0,1},{1,0},{2,3},{3,2},{4,5},{5,4},{6,7},{7,6},{8,9},{9,8},{10,11... | collective-permute-start | bytes 4718600 | tf_op jit(solution)/shard_map/ppermute | solution.py:35
  259.1 41.9 %collective-permute-start.15 = (bf16[4,48,3072]{2,1,0:T(8,128)(2,1)}, bf16[4,48,3072]{2,1,0:T(8,128)(2,1)}, u32[]{:S(2)}, u32[]{:S(2)}) collective-permute-start(bf16[4,48,3072]{2,1,0:T(8,128)(2,1)} %fusion.33), channel_id=1, source_target_pairs={{0,2},{1,5},{2,0},{3,7},{4,6},{5,1},{6,4},{7,3},{8,10},{9,13},{10,... | collective-permute-start | bytes 3538952 | tf_op jit(solution)/shard_map/ppermute | solution.py:31
  262.6 19.2 %collective-permute-start.10 = (bf16[4,48,1536]{2,1,0:T(8,128)(2,1)S(1)}, bf16[4,48,1536]{2,1,0:T(8,128)(2,1)S(1)}, u32[]{:S(2)}, u32[]{:S(2)}) collective-permute-start(bf16[4,48,1536]{2,1,0:T(8,128)(2,1)S(1)} %fusion.77), channel_id=1, source_target_pairs={{0,2},{1,5},{2,0},{3,7},{4,6},{5,1},{6,4},{7,3},{8,10},{9,13},{10,... | collective-permute-start | bytes 1769480 | tf_op jit(solution)/shard_map/ppermute | solution.py:31
  285.3 10.6 %collective-permute-start.13 = (bf16[48,1536]{1,0:T(8,128)(2,1)S(1)}, bf16[48,1536]{1,0:T(8,128)(2,1)S(1)}, u32[]{:S(2)}, u32[]{:S(2)}) collective-permute-start(bf16[48,1536]{1,0:T(8,128)(2,1)S(1)} %get-tuple-element.223), channel_id=1, source_target_pairs={{0,24},{1,25},{2,26},{3,27},{4,28},{5,29},{6,30},{7,31},{8,16},{9,... | collective-permute-start | bytes 442376 | tf_op jit(solution)/shard_map/ppermute | solution.py:31
  287.8 11.9 %collective-permute-start.12 = (bf16[48,1536]{1,0:T(8,128)(2,1)S(1)}, bf16[48,1536]{1,0:T(8,128)(2,1)S(1)}, u32[]{:S(2)}, u32[]{:S(2)}) collective-permute-start(bf16[48,1536]{1,0:T(8,128)(2,1)S(1)} %get-tuple-element.224), channel_id=1, source_target_pairs={{0,16},{1,17},{2,18},{3,19},{4,20},{5,21},{6,22},{7,23},{8,24},{9,... | collective-permute-start | bytes 442376 | tf_op jit(solution)/shard_map/ppermute | solution.py:31
  304.4 13.8 %collective-permute-start.16 = (bf16[48,3072]{1,0:T(8,128)(2,1)S(1)}, bf16[48,3072]{1,0:T(8,128)(2,1)S(1)}, u32[]{:S(2)}, u32[]{:S(2)}) collective-permute-start(bf16[48,3072]{1,0:T(8,128)(2,1)S(1)} %get-tuple-element.209), channel_id=1, source_target_pairs={{0,8},{1,9},{2,10},{3,11},{4,12},{5,13},{6,14},{7,15},{8,0},{9,1},... | collective-permute-start | bytes 884744 | tf_op jit(solution)/shard_map/ppermute | solution.py:31
  304.4 16.7 %collective-permute-start.18 = (bf16[48,3072]{1,0:T(8,128)(2,1)S(1)}, bf16[48,3072]{1,0:T(8,128)(2,1)S(1)}, u32[]{:S(2)}, u32[]{:S(2)}) collective-permute-start(bf16[48,3072]{1,0:T(8,128)(2,1)S(1)} %get-tuple-element.210), channel_id=1, source_target_pairs={{0,24},{1,25},{2,26},{3,27},{4,28},{5,29},{6,30},{7,31},{8,16},{9,... | collective-permute-start | bytes 884744 | tf_op jit(solution)/shard_map/ppermute | solution.py:31
  306.9 25.7 %collective-permute-start.17 = (bf16[48,3072]{1,0:T(8,128)(2,1)S(1)}, bf16[48,3072]{1,0:T(8,128)(2,1)S(1)}, u32[]{:S(2)}, u32[]{:S(2)}) collective-permute-start(bf16[48,3072]{1,0:T(8,128)(2,1)S(1)} %get-tuple-element.211), channel_id=1, source_target_pairs={{0,16},{1,17},{2,18},{3,19},{4,20},{5,21},{6,22},{7,23},{8,24},{9,... | collective-permute-start | bytes 884744 | tf_op jit(solution)/shard_map/ppermute | solution.py:31
  335.3 15.2 %collective-permute-start.26 = (bf16[48,4608]{1,0:T(8,128)(2,1)}, bf16[48,4608]{1,0:T(8,128)(2,1)}, u32[]{:S(2)}, u32[]{:S(2)}) collective-permute-start(bf16[48,4608]{1,0:T(8,128)(2,1)} %pad_maximum_fusion.16), channel_id=1, source_target_pairs={{0,24},{1,25},{2,26},{3,27},{4,28},{5,29},{6,30},{7,31},{8,16},{9,... | collective-permute-start | bytes 1327112 | tf_op jit(solution)/shard_map/ppermute | solution.py:31
  337.6 35.4 %collective-permute-start.25 = (bf16[48,4608]{1,0:T(8,128)(2,1)}, bf16[48,4608]{1,0:T(8,128)(2,1)}, u32[]{:S(2)}, u32[]{:S(2)}) collective-permute-start(bf16[48,4608]{1,0:T(8,128)(2,1)} %pad_maximum_fusion.16), channel_id=1, source_target_pairs={{0,16},{1,17},{2,18},{3,19},{4,20},{5,21},{6,22},{7,23},{8,24},{9,... | collective-permute-start | bytes 1327112 | tf_op jit(solution)/shard_map/ppermute | solution.py:31
  337.6 35.4 %collective-permute-start.24 = (bf16[48,4608]{1,0:T(8,128)(2,1)}, bf16[48,4608]{1,0:T(8,128)(2,1)}, u32[]{:S(2)}, u32[]{:S(2)}) collective-permute-start(bf16[48,4608]{1,0:T(8,128)(2,1)} %pad_maximum_fusion.16), channel_id=1, source_target_pairs={{0,8},{1,9},{2,10},{3,11},{4,12},{5,13},{6,14},{7,15},{8,0},{9,1},... | collective-permute-start | bytes 1327112 | tf_op jit(solution)/shard_map/ppermute | solution.py:31
  375.9 27.5 %collective-permute-start.29 = (bf16[4,48,1536]{2,1,0:T(8,128)(2,1)}, bf16[4,48,1536]{2,1,0:T(8,128)(2,1)S(1)}, u32[]{:S(2)}, u32[]{:S(2)}) collective-permute-start(bf16[4,48,1536]{2,1,0:T(8,128)(2,1)} %get-tuple-element.217), channel_id=1, source_target_pairs={{0,6},{1,7},{2,4},{3,5},{4,2},{5,3},{6,0},{7,1},{8,14},{9,15},{10,... | collective-permute-start | bytes 1769480 | tf_op jit(solution)/shard_map/ppermute | solution.py:31
  376.4 26.9 %collective-permute-start.28 = (bf16[4,48,1536]{2,1,0:T(8,128)(2,1)}, bf16[4,48,1536]{2,1,0:T(8,128)(2,1)}, u32[]{:S(2)}, u32[]{:S(2)}) collective-permute-start(bf16[4,48,1536]{2,1,0:T(8,128)(2,1)} %get-tuple-element.218), channel_id=1, source_target_pairs={{0,4},{1,5},{2,6},{3,7},{4,0},{5,1},{6,2},{7,3},{8,12},{9,13},{10,... | collective-permute-start | bytes 1769480 | tf_op jit(solution)/shard_map/ppermute | solution.py:31
  377.8 25.6 %collective-permute-start.27 = (bf16[4,48,1536]{2,1,0:T(8,128)(2,1)}, bf16[4,48,1536]{2,1,0:T(8,128)(2,1)}, u32[]{:S(2)}, u32[]{:S(2)}) collective-permute-start(bf16[4,48,1536]{2,1,0:T(8,128)(2,1)} %get-tuple-element.219), channel_id=1, source_target_pairs={{0,2},{1,3},{2,0},{3,1},{4,6},{5,7},{6,4},{7,5},{8,10},{9,11},{10,... | collective-permute-start | bytes 1769480 | tf_op jit(solution)/shard_map/ppermute | solution.py:31
  379.4 22.3 %collective-permute-start.19 = (f32[64,128]{1,0:T(8,128)S(1)}, f32[64,128]{1,0:T(8,128)S(1)}, u32[]{:S(2)}, u32[]{:S(2)}) collective-permute-start(f32[64,128]{1,0:T(8,128)S(1)} %pad_bitcast_fusion), channel_id=1, source_target_pairs={{0,2},{1,3},{2,0},{3,1},{4,6},{5,7},{6,4},{7,5},{8,10},{9,11},{10,... | collective-permute-start | bytes 98312 | tf_op jit(solution)/shard_map/ppermute | solution.py:31
  406.9 16.7 %collective-permute-start.30 = (bf16[768,1536]{1,0:T(8,128)(2,1)}, bf16[768,1536]{1,0:T(8,128)(2,1)}, u32[]{:S(2)}, u32[]{:S(2)}) collective-permute-start(bf16[768,1536]{1,0:T(8,128)(2,1)} %bitcast_select_fusion), channel_id=1, source_target_pairs={{0,1},{1,0},{2,3},{3,2},{4,5},{5,4},{6,7},{7,6},{8,9},{9,8},{10,11... | collective-permute-start | bytes 7077896 | tf_op jit(solution)/shard_map/ppermute | solution.py:35
  (131 other events, 1451.4 us)
Sparse Core Ops, SparseCore 0:
  28.1 81.6 all-gather.1

commit v2 on v1

v2 whole, which is shorter than its diff:
```python
import functools
import math

import jax
import jax.numpy as jnp
from jax import lax
from jax.experimental import pallas as pl
from jax.experimental.pallas import tpu as pltpu
from jax.sharding import PartitionSpec as P

D = 768
DH = 64
FF = 3072
NS_ITERS = 5


EPS = 1e-06
NS_A = 3.4445
NS_B = -4.775
NS_C = 2.0315
BF = jnp.bfloat16
F32 = jnp.float32
BOTH = ("dp", "tensor")


def exchange(block, flip_zero, flip_one, wanted=None):
    pairs = []
    for place in range(lax.axis_size("dp")):
        for core, flip in enumerate((flip_zero, flip_one)):
            if wanted is None or (place ^ flip) % 4 in wanted:
                pairs.append((2 * place + core, 2 * (place ^ flip) + core))
    return lax.ppermute(block, BOTH, pairs)


def swap_cores(block):
    return lax.ppermute(block, "tensor", [(0, 1), (1, 0)])


def pick(stack, index):
    return lax.dynamic_index_in_dim(stack, index, 0, keepdims=False)


def gather_rows(block):
    if lax.axis_size("dp") != 16:
        return lax.all_gather(block, "dp", axis=0, tiled=True)
    rows, columns = block.shape
    place = lax.axis_index("dp")
    inner, outer = place % 4, place // 4
    first = lax.axis_index("tensor") == 0
    pieces = jnp.stack([block] + [exchange(block, 4 * d, 4 * d) for d in (1, 2, 3)])
    own = jnp.stack([pick(pieces, outer ^ d) for d in range(4)])
    turned = exchange(own, 2, 1)
    both = exchange(jnp.stack([own, turned]), 1, 2)
    flip_one = jnp.where(first, both[0], turned)
    flip_two = jnp.where(first, turned, both[0])
    groups = jnp.stack([own, flip_one, flip_two, both[1]])
    placed = jnp.stack([pick(groups, inner ^ j) for j in range(4)], axis=1)
    return placed.reshape(16 * rows, columns)


def scatter_order():
    if lax.axis_size("dp") != 16:
        return jnp.arange(16, dtype=jnp.int32)
    inner = lax.axis_index("dp") % 4
    near = jnp.where(lax.axis_index("tensor") == 0, 2, 1)
    flips = jnp.stack([near, near * 0 + 3, near * 0, 3 - near])
    return ((inner ^ flips)[:, None] + 4 * jnp.arange(4)[None, :]).reshape(16).astype(jnp.int32)


def whole_sum(send, keep):
    whole = jnp.concatenate([send.astype(F32), keep]).reshape(-1, send.shape[-1])
    return lax.psum_scatter(whole, "dp", scatter_dimension=0, tiled=True)


def second_parts(keep, got):
    half = keep + got.astype(F32)
    return half[4:].astype(BF), half[:4]


def plane_parts(keep, got):
    outer = lax.axis_index("dp") // 4
    plane = keep + got.astype(F32)
    return [pick(plane, outer ^ d).astype(BF) for d in (1, 2, 3)], pick(plane, outer)


def over_planes(parts):
    return [exchange(part, 4 * d, 4 * d) for d, part in zip((1, 2, 3), parts)]


def add_all(own, parts):
    for part in parts:
        own = own + part.astype(F32)
    return own


def after(value, *others):
    return lax.optimization_barrier((value, *others))[0]


def sum_everywhere(block):
    return jnp.sum(lax.all_gather(block, BOTH, axis=0).reshape(-1, 2, *block.shape), axis=0)


def eye_block(first_row, rows, columns):
    row = lax.broadcasted_iota(jnp.int32, (rows, columns), 0) + first_row
    return row == lax.broadcasted_iota(jnp.int32, (rows, columns), 1)


def nn(left, right):
    return lax.dot_general(left, right, (((1,), (0,)), ((), ())), preferred_element_type=F32)


def nt(left, right):
    return lax.dot_general(left, right, (((1,), (1,)), ((), ())), preferred_element_type=F32)


def ns_kernel(x_ref, t_ref, o_ref, y_ref, a_ref, ab_ref, p_ref, pb_ref, r_ref, rb_ref, col_ref, row_ref):
    blk = 256
    steps = D // blk
    columns = x_ref.shape[1]
    chunk = 768
    half_chunks = columns // chunk

    def put(full_ref, half_ref, slot, i, value):
        rows = pl.ds(pl.multiple_of(i * blk, blk), blk)
        eye = eye_block(i * blk, blk, D)
        only = jnp.where(eye, value, 0.0)
        full_ref[rows, :] = value
        half_ref[rows, :] = jnp.where(eye, 0.0, value).astype(BF)
        col_ref[slot, rows, :] = jnp.sum(only, axis=1, keepdims=True)
        part = jnp.sum(only, axis=0, keepdims=True)

        @pl.when(i == 0)
        def _():
            row_ref[slot] = part

        @pl.when(i > 0)
        def _():
            row_ref[slot] = row_ref[slot] + part

    def gram(sources):
        def outer(i, carry):
            rows = pl.ds(pl.multiple_of(i * blk, blk), blk)
            total = None
            for src, at in sources:
                part = nt(src[rows, at : at + chunk], src[:, at : at + chunk])
                total = part if total is None else total + part
            r_ref[rows, :] = total
            return carry

        lax.fori_loop(0, steps, outer, 0)

    def keep_gram(scale):
        def step(i, carry):
            rows = pl.ds(pl.multiple_of(i * blk, blk), blk)
            put(a_ref, ab_ref, 0, i, r_ref[rows, :] * scale)
            return carry

        lax.fori_loop(0, steps, step, 0)

    def polynomial(turn):
        def step(i, carry):
            rows = pl.ds(pl.multiple_of(i * blk, blk), blk)
            eye = eye_block(i * blk, blk, D)
            dcol, drow = col_ref[0, rows, :], row_ref[0]
            square = nn(ab_ref[rows, :], ab_ref[...])
            value = NS_C * square + a_ref[rows, :] * (NS_B + NS_C * (dcol + drow))
            value = value + jnp.where(eye, NS_A - NS_C * dcol * dcol, 0.0)
            put(p_ref, pb_ref.at[turn], 2 + turn, i, value)
            return carry

        lax.fori_loop(0, steps, step, 0)

    def times(left, left_half, lslot, right, right_half, rslot, out, out_half, oslot):
        def step(i, carry):
            rows = pl.ds(pl.multiple_of(i * blk, blk), blk)
            eye = eye_block(i * blk, blk, D)
            lcol, rrow = col_ref[lslot, rows, :], row_ref[rslot]
            value = nn(left_half[rows, :], right_half[...])
            value = value + lcol * right[rows, :] + left[rows, :] * rrow
            value = value - jnp.where(eye, lcol * rrow, 0.0)
            put(out, out_half, oslot, i, value)
            return carry

        lax.fori_loop(0, steps, step, 0)

    gram([(ref, k * chunk) for ref in (x_ref, t_ref) for k in range(half_chunks)])

    def trace_step(i, total):
        rows = pl.ds(pl.multiple_of(i * blk, blk), blk)
        return total + jnp.sum(jnp.where(eye_block(i * blk, blk, D), r_ref[rows, :], 0.0))

    trace = lax.fori_loop(0, steps, trace_step, jnp.float32(0.0))
    root = jnp.sqrt(jnp.full((1, 1), trace, F32)) + 1e-07
    keep_gram(1.0 / (root * root))
    polynomial(0)
    inverse = 1.0 / root

    def apply_step(i, carry):
        rows = pl.ds(pl.multiple_of(i * blk, blk), blk)
        for k in range(2 * half_chunks):
            src = x_ref if k < half_chunks else t_ref
            at = (k % half_chunks) * chunk
            value = nn(pb_ref[0, rows, :], src[:, at : at + chunk])
            value = value + col_ref[2, rows, :] * src[rows, at : at + chunk].astype(F32)
            y_ref[rows, k * chunk : (k + 1) * chunk] = (value * inverse).astype(BF)
        return carry

    lax.fori_loop(0, steps, apply_step, 0)
    gram([(y_ref, k * chunk) for k in range(2 * half_chunks)])
    keep_gram(1.0)

    def turn_body(turn, carry):
        polynomial(turn)
        times(p_ref, pb_ref.at[turn], 2 + turn, a_ref, ab_ref, 0, r_ref, rb_ref, 1)
        times(r_ref, rb_ref, 1, p_ref, pb_ref.at[turn], 2 + turn, a_ref, ab_ref, 0)
        return carry

    lax.fori_loop(1, NS_ITERS - 1, turn_body, 0)
    polynomial(NS_ITERS - 1)

    wanted = o_ref.shape[0]
    eye = eye_block(0, wanted, D)
    r_ref[:wanted, :] = p_ref[:wanted, :]

    def chain(step, carry):
        turn = NS_ITERS - 2 - step
        left = r_ref[:wanted, :]
        only = jnp.where(eye, left, 0.0)
        lcol = jnp.sum(only, axis=1, keepdims=True)
        off = left - only
        right_half = pb_ref[turn]
        drow = row_ref[2 + turn]
        value = nn(off.astype(BF), right_half)
        value = value + lcol * right_half[:wanted, :].astype(F32) + left * drow
        r_ref[:wanted, :] = value
        return carry

    lax.fori_loop(0, NS_ITERS - 2, chain, 0)
    left = r_ref[:wanted, :]
    only = jnp.where(eye, left, 0.0)
    lcol = jnp.sum(only, axis=1, keepdims=True)
    off = (left - only).astype(BF)
    kept = o_ref.shape[1]
    for k in range(kept // chunk):
        cols = slice(k * chunk, (k + 1) * chunk)
        value = nn(off, y_ref[:, cols]) + lcol * y_ref[:wanted, cols].astype(F32)
        o_ref[:, cols] = value.astype(BF)


def orthogonal_rows(mine, other, wanted):
    vmem = pl.BlockSpec(memory_space=pltpu.VMEM)
    columns = mine.shape[1]
    return pl.pallas_call(
        ns_kernel,
        out_shape=jax.ShapeDtypeStruct((wanted, columns), BF),
        in_specs=[vmem, vmem],
        out_specs=vmem,
        scratch_shapes=[
            pltpu.VMEM((D, 2 * columns), BF),
            pltpu.VMEM((D, D), F32),
            pltpu.VMEM((D, D), BF),
            pltpu.VMEM((D, D), F32),
            pltpu.VMEM((NS_ITERS, D, D), BF),
            pltpu.VMEM((D, D), F32),
            pltpu.VMEM((D, D), BF),
            pltpu.VMEM((2 + NS_ITERS, D, 1), F32),
            pltpu.VMEM((2 + NS_ITERS, 1, D), F32),
        ],
        compiler_params=pltpu.CompilerParams(vmem_limit_bytes=40 * 1024 * 1024),
        cost_estimate=pl.CostEstimate(flops=30 * D**3 * 2, bytes_accessed=4 * mine.size, transcendentals=0),
        name="newton_schulz",
    )(mine, other)


def plane_columns(parts, starts, wide):
    inner = lax.axis_index("dp") % 4
    wanted = [k for k in range(4) if starts[k] is not None]
    table = jnp.array([0 if at is None else at for at in starts], jnp.int32)
    stacked = jnp.stack(parts)

    def columns_of(which):
        return lax.dynamic_slice_in_dim(stacked, pick(table, which), wide, 2)

    return [columns_of(inner)] + [exchange(columns_of(inner ^ d), d, d, wanted) for d in (1, 2, 3)]


def own_matrix(first, last, widths):
    inner = lax.axis_index("dp") % 4
    rows = first[0].shape[0]
    early_wide, late_wide = widths[0], widths[2]
    if lax.axis_size("dp") == 16:
        early = plane_columns(first, [0, widths[1], None, None], early_wide)
        late = plane_columns(last, [None, None, 0, late_wide], late_wide)
        early, late = jnp.stack(early, axis=1), jnp.stack(late, axis=1)
    else:
        count = lax.axis_size("dp")
        turn = (jnp.arange(count) + lax.axis_index("dp") // 4 * 4) % count
        turn = jnp.concatenate([turn[:4][jnp.arange(4) ^ inner], turn[4:]])
        early = lax.all_gather(first[0], "dp")[turn]
        late = lax.all_gather(last[0], "dp")[turn]
        early = lax.dynamic_slice_in_dim(early, (inner & 1) * widths[1], early_wide, 2)
        late = lax.dynamic_slice_in_dim(late, (inner & 1) * late_wide, late_wide, 2)
    column = jnp.arange(early_wide)
    early = jnp.where((inner == 0) | (column >= early_wide - widths[1]), early, jnp.zeros_like(early))
    early = early.reshape(-1, early_wide)
    early = jnp.pad(early, ((0, 0), (0, late_wide - early_wide)))
    return jnp.where(inner < 2, early, late.reshape(-1, late_wide))


def rows_of_all(block, rows):
    inner = lax.axis_index("dp") % 4
    parts = [block[:rows]]
    for d in (1, 2, 3):
        parts.append(exchange(block[d * rows : (d + 1) * rows], d, d))
    parts = jnp.stack(parts)
    return [pick(parts, inner ^ j).astype(F32) for j in range(4)]


def layer_norm(values_in, gain_row, shift_row):
    row_mean = jnp.mean(values_in, axis=-1, keepdims=True)
    centred = values_in - row_mean
    row_var = jnp.mean(centred * centred, axis=-1, keepdims=True)
    return centred * lax.rsqrt(row_var + EPS) * gain_row + shift_row


QB = 256


def tn(left, right):
    return lax.dot_general(left, right, (((0,), (0,)), ((), ())), preferred_element_type=F32)


def rows_at(i):
    return pl.ds(pl.multiple_of(i * QB, QB), QB)


def lanes_at(h):
    return pl.ds(pl.multiple_of(h * 128, 128), 128)


def centre(v):
    c = v - jnp.mean(v, axis=-1, keepdims=True)
    return c, lax.rsqrt(jnp.mean(c * c, axis=-1, keepdims=True) + EPS)


def head_blocks(value, swapped=False):
    a = lax.broadcasted_iota(jnp.int32, (128, 128), 0) // DH
    b = lax.broadcasted_iota(jnp.int32, (128, 128), 1) // DH
    return jnp.where((a != b) if swapped else (a == b), value, 0.0).astype(BF)


def spread(v, blocks):
    high = v.astype(BF)
    low = (v - high.astype(F32)).astype(BF)
    return nn(high, blocks) + nn(low, blocks)


def three_parts(v, lane, first):
    high = v.astype(BF).astype(F32)
    rest = v - high
    low = rest.astype(BF).astype(F32)
    last = rest - low
    return jnp.where(lane == first, high, jnp.where(lane == first + 1, low, last))


def forward_kernel(bounds, x_ref, w_ref, ln_ref, qb_ref, hd_ref, fq_ref, fk_ref,
                   a_ref, qa_ref, ka_ref, va_ref, ob_ref, xh_ref, rs_ref, part_ref, acc_ref):
    half = w_ref.shape[1] // 4
    pairs = half // 128
    blocks = x_ref.shape[0] // QB

    def project(i, carry):
        rows = rows_at(i)
        centred, scale = centre(x_ref[rows, :].astype(F32))
        low = (centred * scale * ln_ref[0:1, :] + ln_ref[1:2, :]).astype(BF)
        a_ref[rows, :] = low
        lane = lax.broadcasted_iota(jnp.int32, (QB, 128), 1)
        mean_blocks = head_blocks(1.0 / DH)
        fq, fk = fq_ref[rows, :].astype(F32), fk_ref[rows, :].astype(F32)
        for t in range(2 * pairs):
            cols = slice(128 * t, 128 * (t + 1))
            raw = nn(low, w_ref[:, cols]) + qb_ref[:, cols]
            raw = raw - spread(raw, mean_blocks)
            scale = lax.rsqrt(spread(raw * raw, mean_blocks) + EPS)
            normal = raw * scale
            xh_ref[rows, cols] = normal.astype(BF)
            rs_ref[rows, cols] = scale.astype(BF)
            out = normal * hd_ref[0:1, cols] + hd_ref[1:2, cols]
            extra, dst, p = (fq, qa_ref, t) if t < pairs else (fk, ka_ref, t - pairs)
            dst[rows, 256 * p : 256 * p + 128] = jnp.where(lane < DH, out, extra).astype(BF)
            dst[rows, 256 * p + 128 : 256 * p + 256] = jnp.where(lane < DH, extra, out).astype(BF)
        for p in range(pairs):
            cols = slice(2 * half + 128 * p, 2 * half + 128 * (p + 1))
            value = nn(low, w_ref[:, cols]) + qb_ref[:, cols]
            va_ref[rows, 256 * p : 256 * p + 128] = jnp.where(lane < DH, value, 1.0).astype(BF)
            va_ref[rows, 256 * p + 128 : 256 * p + 256] = jnp.where(lane < DH, 1.0, value).astype(BF)
        return carry

    lax.fori_loop(0, blocks, project, 0)

    def attend(i, carry):
        rows = rows_at(i)
        acc_ref[...] = jnp.zeros_like(acc_ref)

        def keys(j, carry):
            krows = rows_at(j)
            for h in range(2 * pairs):
                cols = slice(128 * h, 128 * (h + 1))
                weight = jnp.exp(nt(qa_ref[rows, cols], ka_ref[krows, cols])).astype(BF)
                acc_ref[:, cols] = acc_ref[:, cols] + nn(weight, va_ref[krows, cols])
            return carry

        lax.fori_loop(bounds[0, i], bounds[1, i], keys, 0)
        lane = lax.broadcasted_iota(jnp.int32, (QB, 128), 1)
        local = lane % DH
        for p in range(pairs):
            parts = []
            for k in range(2):
                cols = slice(256 * p + 128 * k, 256 * p + 128 * (k + 1))
                acc = acc_ref[:, cols]
                parts.append(acc / pltpu.roll(acc, DH, 1))
                total = three_parts(jnp.log(acc), local, 5)
                other = (lane >= DH) if k == 0 else (lane < DH)
                slot = other & (local >= 5) & (local < 8)
                qa_ref[rows, cols] = jnp.where(slot, total, qa_ref[rows, cols].astype(F32)).astype(BF)
            ob_ref[rows, 128 * p : 128 * (p + 1)] = jnp.where(lane < DH, parts[0], parts[1]).astype(BF)
        part_ref[rows, :] = nt(ob_ref[rows, :], w_ref[:, 3 * half :]).astype(BF)
        return carry

    lax.fori_loop(0, blocks, attend, 0)


def split_rows(order, full_ref, cols, send_ref, keep_ref):
    rows = full_ref.shape[0] // 16

    def move(k, carry):
        src = pl.ds(pl.multiple_of(order[k] * rows, 16), rows)
        send_ref[k, :, cols] = full_ref[src, :].astype(BF)
        src = pl.ds(pl.multiple_of(order[k + 8] * rows, 16), rows)
        keep_ref[k, :, cols] = full_ref[src, :]
        return carry

    lax.fori_loop(0, 8, move, 0)


def long_tn(left_ref, right_ref, out_ref):
    columns = right_ref.shape[1]
    chunk = 384

    def outer(i, carry):
        def inner(k, carry):
            cols = pl.ds(pl.multiple_of(k * chunk, 128), chunk)
            out_ref[rows_at(i), cols] = tn(left_ref[:, rows_at(i)], right_ref[:, cols])
            return carry

        return lax.fori_loop(0, columns // chunk, inner, carry)

    lax.fori_loop(0, left_ref.shape[1] // QB, outer, 0)


def mlp_kernel(order, x_ref, own_ref, got_ref, w_ref, hb_ref, ln_ref, gy_ref,
               h_ref, m_ref, gn_ref, gb_ref, send_ref, keep_ref, a_ref, act_ref, gp_ref, full_ref):
    hidden = w_ref.shape[1] // 2
    chunk = hidden // 2
    blocks = x_ref.shape[0] // QB
    gb_ref[...] = jnp.zeros_like(gb_ref)

    def block(i, carry):
        rows = rows_at(i)
        resid = x_ref[rows, :].astype(F32) + (own_ref[rows, :].astype(F32) + got_ref[rows, :].astype(F32))
        resid = resid + ln_ref[2:3, :]
        h_ref[rows, :] = resid
        centred, scale = centre(resid)
        low = (centred * scale * ln_ref[0:1, :] + ln_ref[1:2, :]).astype(BF)
        a_ref[rows, :] = low
        grad = gy_ref[rows, :]
        out = None
        back = None
        for k in range(2):
            cols = slice(k * chunk, (k + 1) * chunk)
            dcols = slice(hidden + k * chunk, hidden + (k + 1) * chunk)
            pre = nn(low, w_ref[:, cols]) + hb_ref[:, cols]
            square = pre * pre
            inner = math.sqrt(2 / math.pi) * pre * (1.0 + 0.044715 * square)
            tanh = jnp.tanh(inner)
            act = (0.5 * pre * (1.0 + tanh)).astype(BF)
            slope = 0.5 * (1.0 + tanh) + (0.5 * math.sqrt(2 / math.pi)) * pre * (1.0 - tanh * tanh) * (
                1.0 + (3 * 0.044715) * square
            )
            act_ref[rows, cols] = act
            gpre = nn(grad, w_ref[:, dcols]) * slope
            gb_ref[:, cols] = gb_ref[:, cols] + jnp.sum(gpre, axis=0, keepdims=True)
            glow = gpre.astype(BF)
            gp_ref[rows, cols] = glow
            term = nt(act, w_ref[:, dcols])
            out = term if out is None else out + term
            term = nt(glow, w_ref[:, cols])
            back = term if back is None else back + term
        m_ref[rows, :] = out.astype(BF)
        gn_ref[rows, :] = back.astype(BF)
        return carry

    lax.fori_loop(0, blocks, block, 0)
    long_tn(a_ref, gp_ref, full_ref)
    split_rows(order, full_ref, slice(0, hidden), send_ref, keep_ref)
    long_tn(gy_ref, act_ref, full_ref)
    split_rows(order, full_ref, slice(hidden, 2 * hidden), send_ref, keep_ref)


def attention_backward_kernel(bounds, own_ref, got_ref, h_ref, gy_ref, ln_ref, w_ref,
                              qa_ref, ka_ref, va_ref, ob_ref,
                              gh_ref, low_ref, vec_ref, gr_ref, ga_ref, gq_ref, gk_ref, gv_ref):
    half = w_ref.shape[1] // 4
    pairs = half // 128
    blocks = h_ref.shape[0] // QB
    for ref in (vec_ref, gk_ref, gv_ref, gq_ref):
        ref[...] = jnp.zeros_like(ref)

    def second_norm(i, carry):
        rows = rows_at(i)
        grad = own_ref[rows, :].astype(F32) + got_ref[rows, :].astype(F32)
        centred, scale = centre(h_ref[rows, :])
        normal = centred * scale
        gain = grad * ln_ref[0:1, :]
        inner = gain - jnp.mean(gain, axis=-1, keepdims=True)
        inner = inner - normal * jnp.mean(gain * normal, axis=-1, keepdims=True)
        grad_y = gy_ref[rows, :].astype(F32)
        total = grad_y + scale * inner
        gh_ref[rows, :] = total
        for k, item in enumerate((grad * normal, grad, total, grad_y)):
            vec_ref[k : k + 1, :] = vec_ref[k : k + 1, :] + jnp.sum(item, axis=0, keepdims=True)
        low = total.astype(BF)
        low_ref[rows, :] = low
        lane = lax.broadcasted_iota(jnp.int32, (QB, 128), 1)
        local = lane % DH
        cross = head_blocks(1.0, swapped=True)
        for p in range(pairs):
            cols = slice(128 * p, 128 * (p + 1))
            mixed = nn(low, w_ref[:, 3 * half + 128 * p : 3 * half + 128 * (p + 1)]).astype(BF).astype(F32)
            dot = spread(mixed * ob_ref[rows, cols].astype(F32), cross)
            extra = jnp.where(local < 3, three_parts(-dot, local, 0), 0.0)
            ga_ref[rows, 256 * p : 256 * p + 128] = jnp.where(lane < DH, mixed, extra).astype(BF)
            ga_ref[rows, 256 * p + 128 : 256 * p + 256] = jnp.where(lane < DH, extra, mixed).astype(BF)
        return carry

    lax.fori_loop(0, blocks, second_norm, 0)

    def attend(i, carry):
        rows = rows_at(i)

        def keys(j, carry):
            krows = rows_at(j)
            for h in range(2 * pairs):
                cols = slice(128 * h, 128 * (h + 1))
                query, key, out = qa_ref[rows, cols], ka_ref[krows, cols], ga_ref[rows, cols]
                prob = jnp.exp(nt(key, query))
                score = (prob * nt(va_ref[krows, cols], out)).astype(BF)
                gv_ref[krows, cols] = gv_ref[krows, cols] + nn(prob.astype(BF), out)
                gk_ref[krows, cols] = gk_ref[krows, cols] + nn(score, query)
                gq_ref[rows, cols] = gq_ref[rows, cols] + tn(score, key)
            return carry

        return lax.fori_loop(bounds[0, i], bounds[1, i], keys, carry)

    lax.fori_loop(0, blocks, attend, 0)

    def gather(i, carry):
        rows = rows_at(i)
        lane = lax.broadcasted_iota(jnp.int32, (QB, 128), 1)
        for t in range(3 * pairs):
            p = t % pairs
            src = (gq_ref, gk_ref, gv_ref)[t // pairs]
            grad = jnp.where(
                lane < DH, src[rows, 256 * p : 256 * p + 128], src[rows, 256 * p + 128 : 256 * p + 256]
            )
            gr_ref[rows, 128 * t : 128 * (t + 1)] = grad.astype(BF)
        return carry

    lax.fori_loop(0, blocks, gather, 0)


def projection_backward_kernel(order, g_ref, low_ref, ob_ref, w_ref, hd_ref, a_ref, xh_ref, rs_ref,
                               gn_ref, gqb_ref, hv_ref, send_ref, keep_ref, gr_ref, full_ref):
    half = w_ref.shape[1] // 4
    pairs = half // 128
    blocks = g_ref.shape[0] // QB
    for ref in (gqb_ref, hv_ref):
        ref[...] = jnp.zeros_like(ref)

    def head_norm(i, carry):
        rows = rows_at(i)
        mean_blocks = head_blocks(1.0 / DH)
        for t in range(3 * pairs):
            cols = slice(128 * t, 128 * (t + 1))
            grad = g_ref[rows, cols].astype(F32)
            if t < 2 * pairs:
                normal = xh_ref[rows, cols].astype(F32)
                hv_ref[0:1, cols] = hv_ref[0:1, cols] + jnp.sum(grad * normal, axis=0, keepdims=True)
                hv_ref[1:2, cols] = hv_ref[1:2, cols] + jnp.sum(grad, axis=0, keepdims=True)
                gain = grad * hd_ref[0:1, cols]
                inner = gain - spread(gain, mean_blocks) - normal * spread(gain * normal, mean_blocks)
                grad = inner * rs_ref[rows, cols].astype(F32)
            gqb_ref[:, cols] = gqb_ref[:, cols] + jnp.sum(grad, axis=0, keepdims=True)
            gr_ref[rows, cols] = grad.astype(BF)
        gn_ref[rows, :] = nt(gr_ref[rows, :], w_ref[:, : 3 * half]).astype(BF)
        return carry

    lax.fori_loop(0, blocks, head_norm, 0)
    long_tn(a_ref, gr_ref, full_ref.at[:, : 3 * half])
    long_tn(low_ref, ob_ref, full_ref.at[:, 3 * half :])
    split_rows(order, full_ref, slice(0, 4 * half), send_ref, keep_ref)


def call_kernel(kernel, name, scalars, arrays, outs, scratch, flops):
    vmem = pl.BlockSpec(memory_space=pltpu.VMEM)
    smem = pl.BlockSpec(memory_space=pltpu.SMEM)
    size = sum(a.size * a.dtype.itemsize for a in arrays)
    held = size + sum(math.prod(shape) * jnp.dtype(dtype).itemsize for shape, dtype in outs + scratch)
    return pl.pallas_call(
        kernel,
        out_shape=[jax.ShapeDtypeStruct(shape, dtype) for shape, dtype in outs],
        in_specs=[smem] * len(scalars) + [vmem] * len(arrays),
        out_specs=[vmem] * len(outs),
        scratch_shapes=[pltpu.VMEM(shape, dtype) for shape, dtype in scratch],
        compiler_params=pltpu.CompilerParams(vmem_limit_bytes=min(62, held * 5 // 4 // 2**20 + 5) * 2**20),
        cost_estimate=pl.CostEstimate(flops=flops, bytes_accessed=2 * size, transcendentals=0),
        name=name,
    )(*scalars, *arrays)


def body(
    tokens,
    cotangent,
    image_ids,
    step_rates,
    w_qkv,
    w_out,
    w_up,
    w_down,
    norm_gains,
    row_biases,
    head_gains,
    query_bias,
    qkv_bias,
    hidden_bias,
    mom_qkv,
    mom_out,
    mom_up,
    mom_down,
    mom_gains,
    mom_biases,
    mom_head_gains,
    mom_query_bias,
    mom_qkv_bias,
    mom_hidden_bias,
):
    dp_count = lax.axis_size("dp")
    seq_count, length, model_width = tokens.shape
    row_count = seq_count * length
    shard_rows = w_qkv.shape[0]
    half_width = w_qkv.shape[2]
    hidden_part = w_up.shape[1]
    heads_part = half_width // DH
    widths = [3 * half_width, half_width, hidden_part, hidden_part]
    starts = [0, widths[0], widths[0] + widths[1], widths[0] + widths[1] + widths[2]]
    low_weights = jnp.concatenate(
        [w_qkv.reshape(shard_rows, 3 * half_width), w_out.T, w_up, w_down.T], axis=1
    ).astype(BF)
    first_weights = gather_rows(low_weights[:, : starts[2]])
    last_weights = lax.all_gather(low_weights[:, starts[2] :], "dp", axis=0, tiled=True)
    x_low = tokens.reshape(row_count, model_width)
    grad_low = cotangent.reshape(row_count, model_width)
    ids = image_ids.reshape(row_count)
    less = jnp.sum(ids[None, :] < jnp.arange(5)[:, None], axis=1)
    heads_of = ids[::QB]
    tails_of = ids[QB - 1 :: QB]
    bounds = jnp.stack([less[heads_of] // QB, (less[tails_of + 1] + QB - 1) // QB]).astype(jnp.int32)
    local = jnp.arange(128)[None, :] % DH
    hot = jnp.where(ids[:, None] == local, 16.0, 0.0)
    for_query = jnp.where(local == 4, -16.0, hot).astype(BF)
    for_key = jnp.where(local == 4, 16.0, jnp.where((local > 4) & (local < 8), -1.0, hot)).astype(BF)
    scale = DH**-0.5
    pad = jnp.zeros((half_width,), F32)
    head_rows = jnp.stack(
        [
            jnp.concatenate([jnp.tile(head_gains[0] * scale, heads_part), jnp.tile(head_gains[1], heads_part)]),
            jnp.concatenate([jnp.tile(query_bias * scale, heads_part), pad]),
        ]
    )
    order = scatter_order()
    wide = (row_count, 2 * half_width)
    full = (row_count, model_width)
    normed_one, qa, ka, va, mixed, normal, rscale, attn_part = call_kernel(
        forward_kernel,
        "attention_forward",
        [bounds],
        [
            x_low,
            first_weights,
            jnp.stack([norm_gains[0], row_biases[0]]),
            qkv_bias.reshape(1, 3 * half_width),
            head_rows,
            for_query,
            for_key,
        ],
        [(full, BF), (wide, BF), (wide, BF), (wide, BF), ((row_count, half_width), BF), (wide, BF), (wide, BF), (full, BF)],
        [((QB, 2 * half_width), F32)],
        5 * 10**9,
    )
    attn_got = swap_cores(attn_part)
    residual, mlp_part, part_two, hidden_grad, late_send, late_keep = call_kernel(
        mlp_kernel,
        "mlp",
        [order],
        [
            x_low,
            attn_part,
            attn_got,
            last_weights,
            hidden_bias.reshape(1, hidden_part),
            jnp.stack([norm_gains[1], row_biases[2], row_biases[1]]),
            grad_low,
        ],
        [
            (full, F32),
            (full, BF),
            (full, BF),
            ((1, hidden_part), F32),
            ((8, model_width // 16, 2 * hidden_part), BF),
            ((8, model_width // 16, 2 * hidden_part), F32),
        ],
        [
            (full, BF),
            ((row_count, hidden_part), BF),
            ((row_count, hidden_part), BF),
            ((model_width, hidden_part), F32),
        ],
        15 * 10**9,
    )
    fast = dp_count == 16
    two_got = swap_cores(part_two)
    late_got = exchange(late_send, 2, 1) if fast else None
    grad_resid, resid_low, vectors, heads_grad = call_kernel(
        attention_backward_kernel,
        "attention_backward",
        [bounds],
        [part_two, two_got, residual, grad_low, norm_gains[1:2], first_weights, qa, ka, va, mixed],
        [(full, F32), (full, BF), ((4, model_width), F32), ((row_count, 3 * half_width), BF)],
        [(wide, BF), (wide, F32), (wide, F32), (wide, F32)],
        14 * 10**9,
    )
    if fast:
        late_send, late_keep = second_parts(late_keep, after(late_got, heads_grad))
        order = after(order, late_send)
        late_got = exchange(late_send, 1, 2)
    part_one, grad_qkv_bias_local, head_sums, early_send, early_keep = call_kernel(
        projection_backward_kernel,
        "projection_backward",
        [order],
        [heads_grad, resid_low, mixed, first_weights, head_rows, normed_one, normal, rscale],
        [
            (full, BF),
            ((1, 3 * half_width), F32),
            ((2, 2 * half_width), F32),
            ((8, model_width // 16, 4 * half_width), BF),
            ((8, model_width // 16, 4 * half_width), F32),
        ],
        [((row_count, 3 * half_width), BF), ((model_width, 4 * half_width), F32)],
        8 * 10**9,
    )
    old_first = 0.5 * jnp.concatenate([mom_qkv.reshape(shard_rows, 3 * half_width), mom_out.T], axis=1)
    old_last = 0.5 * jnp.concatenate([mom_up, mom_down.T], axis=1)
    one_got = swap_cores(part_one)
    if fast:
        early_got = exchange(early_send, 2, 1)
        parts, late_own = plane_parts(late_keep, late_got)
        late_parts = over_planes(parts)
        early_send, early_keep = second_parts(early_keep, early_got)
        early_got = exchange(early_send, 1, 2)
        parts, early_own = plane_parts(early_keep, early_got)
        early_parts = over_planes(parts)
        late = add_all(late_own, late_parts)
        last_mom = old_last + late
        last_low = last_mom.astype(BF)
        last_planes = [last_low] + over_planes([last_low] * 3)
        early = add_all(early_own, early_parts)
        first_mom = old_first + early
        first_low = first_mom.astype(BF)
        first_planes = [first_low] + over_planes([first_low] * 3)
    else:
        late, early = whole_sum(late_send, late_keep), whole_sum(early_send, early_keep)
        last_mom, first_mom = old_last + late, old_first + early
        last_planes, first_planes = [last_mom.astype(BF)], [first_mom.astype(BF)]
    mlp_out = mlp_part.astype(F32) + swap_cores(mlp_part).astype(F32) + row_biases[3]
    block_out = (residual + mlp_out).reshape(tokens.shape)
    grad_normed_one = part_one.astype(F32) + one_got.astype(F32)
    _, norm_one_pull = jax.vjp(layer_norm, x_low.astype(F32), norm_gains[0], row_biases[0])
    grad_flat_ln, grad_gain_one, grad_shift_one = norm_one_pull(grad_normed_one)
    tokens_grad = (grad_resid + grad_flat_ln).reshape(tokens.shape)
    head_sums = head_sums.reshape(2, 2, heads_part, DH).sum(axis=2)
    grad_head_local = jnp.stack([head_sums[0, 0] * scale, head_sums[0, 1]])
    grad_qshift_local = head_sums[1, 0] * scale
    grad_rows = [early[:, : starts[1]], early[:, starts[1] :], late[:, :hidden_part], late[:, hidden_part:]]
    grad_qkv = grad_rows[0].reshape(shard_rows, 3, half_width)
    grad_out, grad_up, grad_down = grad_rows[1].T, grad_rows[2], grad_rows[3].T
    next_mom_qkv = first_mom[:, : starts[1]].reshape(shard_rows, 3, half_width)
    next_mom_out = first_mom[:, starts[1] :].T
    next_mom_up, next_mom_down = last_mom[:, :hidden_part], last_mom[:, hidden_part:].T
    matrix = own_matrix(first_planes, last_planes, widths)
    own_rows = rows_of_all(orthogonal_rows(matrix, swap_cores(matrix), 4 * shard_rows), shard_rows)
    small = [
        jnp.stack([grad_gain_one, vectors[0]]),
        jnp.stack([grad_shift_one, vectors[2], vectors[1], vectors[3]]),
        grad_qkv_bias_local.reshape(3, half_width),
        hidden_grad.reshape(hidden_part),
        grad_head_local,
        grad_qshift_local,
    ]
    sizes = [part.size for part in small]
    flat = jnp.concatenate([part.reshape(-1) for part in small])
    flat = jnp.pad(flat, (0, -flat.size % 1024)).reshape(-1, 128)
    by_core = sum_everywhere(flat)
    cut = sum(sizes[:4])
    summed = pick(by_core, lax.axis_index("tensor")).reshape(-1)
    heads = (by_core[0] + by_core[1]).reshape(-1)[cut : cut + sizes[4] + sizes[5]]
    pieces = []
    at = 0
    for part, size in zip(small[:4], sizes):
        pieces.append(summed[at : at + size].reshape(part.shape))
        at += size
    grad_gains, grad_biases, grad_qkv_bias, grad_hidden_bias = pieces
    grad_head_gains = heads[: sizes[4]].reshape(grad_head_local.shape)
    grad_query_bias = heads[sizes[4] :]
    rate_muon = step_rates[0]
    new_w_qkv = w_qkv - rate_muon * (0.2 * math.sqrt(max(D, 3 * D))) * own_rows[0][
        :, : 3 * half_width
    ].reshape(shard_rows, 3, half_width)
    new_w_out = w_out - rate_muon * (0.2 * math.sqrt(D)) * own_rows[1][:, 2 * half_width : 3 * half_width].T
    new_w_up = w_up - rate_muon * (0.2 * math.sqrt(max(D, FF))) * own_rows[2][:, :hidden_part]
    new_w_down = w_down - rate_muon * (0.2 * math.sqrt(max(D, FF))) * own_rows[3][:, :hidden_part].T
    rate_vector = step_rates[1] / math.sqrt(row_count * dp_count)
    next_mom_gains = 0.5 * mom_gains + grad_gains
    next_mom_biases = 0.5 * mom_biases + grad_biases
    next_mom_head_gains = 0.5 * mom_head_gains + grad_head_gains
    next_mom_query_bias = 0.5 * mom_query_bias + grad_query_bias
    next_mom_qkv_bias = 0.5 * mom_qkv_bias + grad_qkv_bias
    next_mom_hidden_bias = 0.5 * mom_hidden_bias + grad_hidden_bias
    new_gains = norm_gains - rate_vector * next_mom_gains
    new_biases = row_biases - rate_vector * next_mom_biases
    new_head_gains = head_gains - rate_vector * next_mom_head_gains
    new_query_bias = query_bias - rate_vector * next_mom_query_bias
    new_qkv_bias = qkv_bias - rate_vector * next_mom_qkv_bias
    new_hidden_bias = hidden_bias - rate_vector * next_mom_hidden_bias
    return (
        block_out,
        tokens_grad,
        grad_qkv,
        grad_out,
        grad_up,
        grad_down,
        grad_gains,
        grad_biases,
        grad_head_gains,
        grad_query_bias,
        grad_qkv_bias,
        grad_hidden_bias,
        next_mom_qkv,
        next_mom_out,
        next_mom_up,
        next_mom_down,
        next_mom_gains,
        next_mom_biases,
        next_mom_head_gains,
        next_mom_query_bias,
        next_mom_qkv_bias,
        next_mom_hidden_bias,
        new_w_qkv,
        new_w_out,
        new_w_up,
        new_w_down,
        new_gains,
        new_biases,
        new_head_gains,
        new_query_bias,
        new_qkv_bias,
        new_hidden_bias,
    )


def solution(mesh):
    return jax.shard_map(
        body,
        mesh=mesh,
        in_specs=(
            P("dp", None, None),
            P("dp", None, None),
            P("dp", None),
            P(),
            P("dp", None, "tensor"),
            P("tensor", "dp"),
            P("dp", "tensor"),
            P("tensor", "dp"),
            P(),
            P(),
            P(),
            P(),
            P(None, "tensor"),
            P("tensor"),
            P("dp", None, "tensor"),
            P("tensor", "dp"),
            P("dp", "tensor"),
            P("tensor", "dp"),
            P(),
            P(),
            P(),
            P(),
            P(None, "tensor"),
            P("tensor"),
        ),
        out_specs=(
            P("dp", None, None),
            P("dp", None, None),
            P("dp", None, "tensor"),
            P("tensor", "dp"),
            P("dp", "tensor"),
            P("tensor", "dp"),
            P(),
            P(),
            P(),
            P(),
            P(None, "tensor"),
            P("tensor"),
            P("dp", None, "tensor"),
            P("tensor", "dp"),
            P("dp", "tensor"),
            P("tensor", "dp"),
            P(),
            P(),
            P(),
            P(),
            P(None, "tensor"),
            P("tensor"),
            P("dp", None, "tensor"),
            P("tensor", "dp"),
            P("dp", "tensor"),
            P("tensor", "dp"),
            P(),
            P(),
            P(),
            P(),
            P(None, "tensor"),
            P("tensor"),
        ),
        check_vma=False,
    )
```

time: 513 us -> 429 us (0.84); the launches traced: 504 us -> 425 us
  matrix products: 97.1 us -> 0 us
  Pallas kernels: 53.2 us -> 144 us
  other arithmetic: 117 us -> 47.3 us
  waiting for transfers between devices: 132 us -> 96.8 us
  starting transfers between devices: 36.1 us -> 66.6 us
  between operations: 26.9 us -> 33.9 us
  local copies, waits for them, and re-layouts: 42.1 us -> 36.9 us
    dot_general x24 -> x0, matrix products: 97.1 us -> none  [the longest x4 19.7 us: dense(): return jnp.dot(left_in, right_in, preferred_element_type=jnp.float32)]
    pallas_call x1 -> x5, Pallas kernels: 53.2 us -> 144 us  [the longest x4 99.5 us: call_kernel(): pl.pallas_call(kernel, out_shape=[jax.ShapeDtypeStruct(shape, dtype) for...]
    ppermute x28 -> x30, waiting for transfers between devices: 132 us -> 91.7 us  [exchange(): return lax.ppermute(block, BOTH, pairs)]
    ppermute x28 -> x30, starting transfers between devices: 35.4 us -> 66 us  [exchange(): return lax.ppermute(block, BOTH, pairs)]
    convert_element_type x8 -> x3, other arithmetic: 28.6 us -> 0.5 us  [the longest x1 0.2 us: body(): jnp.where(local == 4, 16.0, jnp.where((local > 4) & (local < 8), -1.0, hot))]
    concatenate x7 -> x2, other arithmetic: 16.4 us -> 1.32 us  [the longest x1 1.31 us: body(): flat = jnp.concatenate([part.reshape(-1) for part in small])]
    reduce_sum x5 -> x3, other arithmetic: 15.7 us -> 1.43 us  [the longest x1 1.29 us: sum_everywhere(): jnp.sum(lax.all_gather(block, BOTH, axis=0).reshape(-1, 2, *block.shape),...]
    reduce_sum x5 -> x1, other arithmetic: 12.1 us -> 3.75 us  [layer_norm(): return centred * lax.rsqrt(row_var + EPS) * gain_row + shift_row]
  transfers between devices with their start and end apart: 35 -> 37, of which waited for: 18 -> 16; matrix products, arithmetic and copies ran while one was open for 41% -> 14% of each run, Pallas kernels for 0% -> 16%
where the time goes in v2:
time: 429 us; the launch traced here: 425 us
  Pallas kernels  144 us (34%)
  waiting for transfers between devices  96.8 us (23%)
  starting transfers between devices  66.6 us (16%)
  other arithmetic  47.3 us (11%)
  local copies, waits for them, and re-layouts  36.9 us (9%)
  between operations  33.9 us (8%)
    pallas_call x4, Pallas kernels, call_kernel(): pl.pallas_call(kernel, out_shape=[jax.ShapeDtypeStruct(shape, dtype) for...  99.5 us
    ppermute x30, waiting for transfers between devices, exchange(): return lax.ppermute(block, BOTH, pairs)  91.7 us
    ppermute x30, starting transfers between devices, exchange(): return lax.ppermute(block, BOTH, pairs)  66 us
    pallas_call x1, Pallas kernels, orthogonal_rows(): pl.pallas_call(ns_kernel, out_shape=jax.ShapeDtypeStruct((wanted, columns...  44.3 us
    unnamed x135, local copies, waits for them, and re-layouts  21.1 us
  transfers between devices with their start and end apart: 37, of which 16 were waited for; matrix products, arithmetic and copies ran while one was open for 14% of the time, Pallas kernels for 16%

profile of v2, /device:TPU:0, one launch (start us, length us, event | category | flops | bytes accessed | tf_op | source)
XLA Modules:
  0.0 425.3 jit_solution(2303400513460957603)
XLA Ops:
  11.1 5.1 %collective-permute-start.2 = (bf16[48,1536]{1,0:T(8,128)(2,1)S(1)}, bf16[48,1536]{1,0:T(8,128)(2,1)S(1)}, u32[]{:S(2)}, u32[]{:S(2)}) collective-permute-start(bf16[48,1536]{1,0:T(8,128)(2,1)S(1)} %get-tuple-element.272), channel_id=1, source_target_pairs={{0,24},{1,25},{2,26},{3,27},{4,28},{5,29},{6,30},{7,31},{8,16},{9,... | collective-permute-start | bytes 442376 | tf_op jit(solution)/shard_map/ppermute | solution.py:32
  17.3 3.7 collective-permute-done.2
  24.3 8.1 %collective-permute-done.1 = bf16[48,1536]{1,0:T(8,128)(2,1)S(1)} collective-permute-done((bf16[48,1536]{1,0:T(8,128)(2,1)S(1)}, bf16[48,1536]{1,0:T(8,128)(2,1)S(1)}, u32[]{:S(2)}, u32[]{:S(2)}) %collective-permute-start.1) | collective-permute-done | bytes 147488 | tf_op jit(solution)/shard_map/ppermute | solution.py:32
  35.0 7.6 %collective-permute-done.3 = bf16[4,48,1536]{2,1,0:T(8,128)(2,1)S(1)} collective-permute-done((bf16[4,48,1536]{2,1,0:T(8,128)(2,1)S(1)}, bf16[4,48,1536]{2,1,0:T(8,128)(2,1)S(1)}, u32[]{:S(2)}, u32[]{:S(2)}) %collective-permute-start.3) | collective-permute-done | bytes 589856 | tf_op jit(solution)/shard_map/ppermute | solution.py:32
  46.3 20.1 %collective-permute-done.4 = bf16[2,4,48,1536]{3,2,1,0:T(8,128)(2,1)S(1)} collective-permute-done((bf16[2,4,48,1536]{3,2,1,0:T(8,128)(2,1)}, bf16[2,4,48,1536]{3,2,1,0:T(8,128)(2,1)S(1)}, u32[]{:S(2)}, u32[]{:S(2)}) %collective-permute-start.4) | collective-permute-done | bytes 1179680 | tf_op jit(solution)/shard_map/ppermute | solution.py:32
  70.9 22.6 %attention_forward.1 = (bf16[1024,768]{1,0:T(8,128)(2,1)S(1)}, bf16[1024,768]{1,0:T(8,128)(2,1)S(1)}, bf16[1024,768]{1,0:T(8,128)(2,1)S(1)}, bf16[1024,768]{1,0:...) custom-call(s32[2,4]{1,0:T(2,128)S(1)} %pad_add_fusion.bounds, ...), custom_call_target="tpu_custom_call" | custom-call | flops 5000000000 | bytes 8946688 | tf_op jit(solution)/shard_map/attention_forward/pallas_call | solution.py:620
  105.1 33.4 %mlp.1 = (f32[1024,768]{1,0:T(8,128)}, bf16[1024,768]{1,0:T(8,128)(2,1)S(1)}, bf16[1024,768]{1,0:T(8,128)(2,1)}, f32[1,1536]{1,0:T(1,128)S(1)}, bf16[8,48,3072]{2,1,0:T(8,128)(2,1)}, /*index=5*/f32[8,48,3072]{2,1,0:T(8,128)}) custom-call(s32[16]{0:T(128)S(1)} %add.277.order, bf16[1024,768]{1,0:T(8,128)(2,1)S(1)} %bitcast.189, bf16[1024,768]{1,0:T(8,128)(2,1)} %copy-done.6, ...), custom_call_target="tpu_custom_call" | custom-call | flops 15000000512 | bytes 22050816 | tf_op jit(solution)/shard_map/mlp/pallas_call | solution.py:620
  162.1 4.7 %add_bitcast_fusion.1 = f32[1,1024,768]{2,1,0:T(8,128)} fusion(f32[1024,768]{1,0:T(8,128)} %get-tuple-element.58.h_ref, bf16[1024,768]{1,0:T(8,128)(2,1)} %collective-permute-done.6, bf16[1024,768]{1,0:T(8,128)(2,1)S(1)} %get-tuple-element.59, f32[768]{0:T(1024)S(1)} %get-tuple-element.277), kind=kLoop, calls=%fused_computation.16 | loop fusion | flops 3932160 | bytes 9440256 | tf_op jit(solution)/shard_map/reshape | solution.py:796
  166.8 30.4 %attention_backward.1 = (f32[1024,768]{1,0:T(8,128)}, bf16[1024,768]{1,0:T(8,128)(2,1)S(1)}, f32[4,768]{1,0:T(4,128)S(1)}, bf16[1024,1152]{1,0:T(8,128)(2,1)}) custom-call(s32[2,4]{1,0:T(2,128)S(1)} %pad_add_fusion.bounds, bf16[1024,768]{1,0:T(8,128)(2,1)} %get-tuple-element.60.own_ref, bf16[1024,768]{1,0:T(8,128)(2,1)} %collective-permute-done.7.got_ref, ...), custom_call_target="tpu_custom_call" | custom-call | flops 14000000000 | bytes 31463424 | tf_op jit(solution)/shard_map/attention_backward/pallas_call | solution.py:620
  197.2 3.8 convert_add_fusion
  205.3 13.1 %projection_backward.1 = (bf16[1024,768]{1,0:T(8,128)(2,1)S(1)}, f32[1,1152]{1,0:T(1,128)S(1)}, f32[2,768]{1,0:T(2,128)S(1)}, bf16[8,48,1536]{2,1,0:T(8,128)(2,1)}, f32[8,48,1536]{2,1,0:T(8,128)S(1)}) custom-call(s32[16]{0:T(128)S(1)} %add.277.order, bf16[1024,1152]{1,0:T(8,128)(2,1)S(1)} %copy-done.17, bf16[1024,768]{1,0:T(8,128)(2,1)S(1)} %get-tuple-element.71.low_ref, ...), custom_call_target="tpu_custom_call" | custom-call | flops 8000000000 | bytes 23605248 | tf_op jit(solution)/shard_map/projection_backward/pallas_call | solution.py:620
  224.3 12.8 %collective-permute-start.16 = (bf16[48,3072]{1,0:T(8,128)(2,1)S(1)}, bf16[48,3072]{1,0:T(8,128)(2,1)S(1)}, u32[]{:S(2)}, u32[]{:S(2)}) collective-permute-start(bf16[48,3072]{1,0:T(8,128)(2,1)S(1)} %get-tuple-element.235), channel_id=1, source_target_pairs={{0,8},{1,9},{2,10},{3,11},{4,12},{5,13},{6,14},{7,15},{8,0},{9,1},... | collective-permute-start | bytes 884744 | tf_op jit(solution)/shard_map/ppermute | solution.py:32
  244.7 6.0 %collective-permute-done.16 = bf16[48,3072]{1,0:T(8,128)(2,1)S(1)} collective-permute-done((bf16[48,3072]{1,0:T(8,128)(2,1)S(1)}, bf16[48,3072]{1,0:T(8,128)(2,1)S(1)}, u32[]{:S(2)}, u32[]{:S(2)}) %collective-permute-start.16) | collective-permute-done | bytes 294944 | tf_op jit(solution)/shard_map/ppermute | solution.py:32
  250.7 9.9 %collective-permute-done.17 = bf16[48,3072]{1,0:T(8,128)(2,1)S(1)} collective-permute-done((bf16[48,3072]{1,0:T(8,128)(2,1)S(1)}, bf16[48,3072]{1,0:T(8,128)(2,1)S(1)}, u32[]{:S(2)}, u32[]{:S(2)}) %collective-permute-start.17) | collective-permute-done | bytes 294944 | tf_op jit(solution)/shard_map/ppermute | solution.py:32
  260.8 6.5 %collective-permute-start.25 = (bf16[48,3072]{1,0:T(8,128)(2,1)S(1)}, bf16[48,3072]{1,0:T(8,128)(2,1)}, u32[]{:S(2)}, u32[]{:S(2)}) collective-permute-start(bf16[48,3072]{1,0:T(8,128)(2,1)S(1)} %get-tuple-element.232), channel_id=1, source_target_pairs={{0,8},{1,9},{2,10},{3,11},{4,12},{5,13},{6,14},{7,15},{8,0},{9,1},... | collective-permute-start | bytes 884744 | tf_op jit(solution)/shard_map/ppermute | solution.py:32
  274.2 3.7 fusion.7
  298.3 7.8 %collective-permute-done.13 = bf16[48,1536]{1,0:T(8,128)(2,1)S(1)} collective-permute-done((bf16[48,1536]{1,0:T(8,128)(2,1)S(1)}, bf16[48,1536]{1,0:T(8,128)(2,1)S(1)}, u32[]{:S(2)}, u32[]{:S(2)}) %collective-permute-start.13) | collective-permute-done | bytes 147488 | tf_op jit(solution)/shard_map/ppermute | solution.py:32
  314.5 3.8 collective-permute-start.30
  318.3 5.3 %collective-permute-done.20 = bf16[48,1536]{1,0:T(8,128)(2,1)S(1)} collective-permute-done((bf16[48,1536]{1,0:T(8,128)(2,1)S(1)}, bf16[48,1536]{1,0:T(8,128)(2,1)S(1)}, u32[]{:S(2)}, u32[]{:S(2)}) %collective-permute-start.20) | collective-permute-done | bytes 147488 | tf_op jit(solution)/shard_map/ppermute | solution.py:32
  323.8 4.1 collective-permute-start.22
  330.6 4.1 add_bitcast_fusion
  334.6 4.5 %collective-permute-done.29 = bf16[4,48,1536]{2,1,0:T(8,128)(2,1)S(1)} collective-permute-done((bf16[4,48,1536]{2,1,0:T(8,128)(2,1)S(1)}, bf16[4,48,1536]{2,1,0:T(8,128)(2,1)S(1)}, u32[]{:S(2)}, u32[]{:S(2)}) %collective-permute-start.29) | collective-permute-done | bytes 589856 | tf_op jit(solution)/shard_map/ppermute | solution.py:32
  340.0 9.2 %collective-permute-done.23 = bf16[4,48,1152]{2,1,0:T(8,128)(2,1)S(1)} collective-permute-done((bf16[4,48,1152]{2,1,0:T(8,128)(2,1)S(1)}, bf16[4,48,1152]{2,1,0:T(8,128)(2,1)S(1)}, u32[]{:S(2)}, u32[]{:S(2)}) %collective-permute-start.23) | collective-permute-done | bytes 442400 | tf_op jit(solution)/shard_map/ppermute | solution.py:32
  360.3 44.3 %newton_schulz.1 = bf16[192,1536]{1,0:T(8,128)(2,1)S(1)} custom-call(bf16[768,1536]{1,0:T(8,128)(2,1)S(1)} %bitcast_select_fusion.x_ref, bf16[768,1536]{1,0:T(8,128)(2,1)} %collective-permute-done.31.t_ref), custom_call_target="tpu_custom_call" | custom-call | flops 27179089920 | bytes 4718592 | tf_op jit(solution)/shard_map/newton_schulz/pallas_call | solution.py:254
  (325 shorter events, 116.9 us)
Async XLA Ops:
  7.2 97.9 %all-gather.3.cloned.1.call-start = ((), (), s32[]{:S(2)}) async-start(), calls=%async_computation | async-start | bytes 5013504 | tf_op jit(solution)/shard_map/all_gather | solution.py:671
  10.0 345.7 %all-gather.5.cloned.1.call-start = ((), (), s32[]{:S(2)}) async-start(), calls=%async_computation.1 | async-start | bytes 1081344 | tf_op jit(solution)/shard_map/all_gather | solution.py:101
  16.2 16.1 %collective-permute-start.1 = (bf16[48,1536]{1,0:T(8,128)(2,1)S(1)}, bf16[48,1536]{1,0:T(8,128)(2,1)S(1)}, u32[]{:S(2)}, u32[]{:S(2)}) collective-permute-start(bf16[48,1536]{1,0:T(8,128)(2,1)S(1)} %get-tuple-element.272), channel_id=1, source_target_pairs={{0,16},{1,17},{2,18},{3,19},{4,20},{5,21},{6,22},{7,23},{8,24},{9,... | collective-permute-start | bytes 442376 | tf_op jit(solution)/shard_map/ppermute | solution.py:32
  43.7 22.7 %collective-permute-start.4 = (bf16[2,4,48,1536]{3,2,1,0:T(8,128)(2,1)}, bf16[2,4,48,1536]{3,2,1,0:T(8,128)(2,1)S(1)}, u32[]{:S(2)}, u32[]{:S(2)}) collective-permute-start(bf16[2,4,48,1536]{3,2,1,0:T(8,128)(2,1)} %pad_maximum_fusion.4), channel_id=1, source_target_pairs={{0,2},{1,5},{2,0},{3,7},{4,6},{5,1},{6,4},{7,3},{8,10},{9,13},{10,... | collective-permute-start | bytes 3538952 | tf_op jit(solution)/shard_map/ppermute | solution.py:32
  138.5 23.5 %collective-permute-start.6 = (bf16[1024,768]{1,0:T(8,128)(2,1)S(1)}, bf16[1024,768]{1,0:T(8,128)(2,1)}, u32[]{:S(2)}, u32[]{:S(2)}) collective-permute-start(bf16[1024,768]{1,0:T(8,128)(2,1)S(1)} %get-tuple-element.59), channel_id=1, source_target_pairs={{0,1},{1,0},{2,3},{3,2},{4,5},{5,4},{6,7},{7,6},{8,9},{9,8},{10,11... | collective-permute-start | bytes 4718600 | tf_op jit(solution)/shard_map/ppermute | solution.py:36
  138.7 28.1 %collective-permute-start.7 = (bf16[1024,768]{1,0:T(8,128)(2,1)}, bf16[1024,768]{1,0:T(8,128)(2,1)}, u32[]{:S(2)}, u32[]{:S(2)}) collective-permute-start(bf16[1024,768]{1,0:T(8,128)(2,1)} %get-tuple-element.60.own_ref), channel_id=1, source_target_pairs={{0,1},{1,0},{2,3},{3,2},{4,5},{5,4},{6,7},{7,6},{8,9},{9,8},{10,11... | collective-permute-start | bytes 4718600 | tf_op jit(solution)/shard_map/ppermute | solution.py:36
  150.7 46.4 %collective-permute-start.8 = (bf16[8,48,3072]{2,1,0:T(8,128)(2,1)}, bf16[8,48,3072]{2,1,0:T(8,128)(2,1)}, u32[]{:S(2)}, u32[]{:S(2)}) collective-permute-start(bf16[8,48,3072]{2,1,0:T(8,128)(2,1)} %get-tuple-element.67), channel_id=1, source_target_pairs={{0,4},{1,3},{2,6},{3,1},{4,0},{5,7},{6,2},{7,5},{8,12},{9,11},{10,... | collective-permute-start | bytes 7077896 | tf_op jit(solution)/shard_map/ppermute | solution.py:32
  202.3 19.4 %collective-permute-start.15 = (bf16[4,48,3072]{2,1,0:T(8,128)(2,1)}, bf16[4,48,3072]{2,1,0:T(8,128)(2,1)}, u32[]{:S(2)}, u32[]{:S(2)}) collective-permute-start(bf16[4,48,3072]{2,1,0:T(8,128)(2,1)} %slice.285), channel_id=1, source_target_pairs={{0,2},{1,5},{2,0},{3,7},{4,6},{5,1},{6,4},{7,3},{8,10},{9,13},{10,... | collective-permute-start | bytes 3538952 | tf_op jit(solution)/shard_map/ppermute | solution.py:32
  219.8 20.2 %collective-permute-start.10 = (bf16[8,48,1536]{2,1,0:T(8,128)(2,1)}, bf16[8,48,1536]{2,1,0:T(8,128)(2,1)}, u32[]{:S(2)}, u32[]{:S(2)}) collective-permute-start(bf16[8,48,1536]{2,1,0:T(8,128)(2,1)} %get-tuple-element.77), channel_id=1, source_target_pairs={{0,4},{1,3},{2,6},{3,1},{4,0},{5,7},{6,2},{7,5},{8,12},{9,11},{10,... | collective-permute-start | bytes 3538952 | tf_op jit(solution)/shard_map/ppermute | solution.py:32
  221.1 50.3 %collective-permute-start.9 = (bf16[1024,768]{1,0:T(8,128)(2,1)S(1)}, bf16[1024,768]{1,0:T(8,128)(2,1)}, u32[]{:S(2)}, u32[]{:S(2)}) collective-permute-start(bf16[1024,768]{1,0:T(8,128)(2,1)S(1)} %get-tuple-element.75), channel_id=1, source_target_pairs={{0,1},{1,0},{2,3},{3,2},{4,5},{5,4},{6,7},{7,6},{8,9},{9,8},{10,11... | collective-permute-start | bytes 4718600 | tf_op jit(solution)/shard_map/ppermute | solution.py:36
  224.3 26.4 %collective-permute-start.16 = (bf16[48,3072]{1,0:T(8,128)(2,1)S(1)}, bf16[48,3072]{1,0:T(8,128)(2,1)S(1)}, u32[]{:S(2)}, u32[]{:S(2)}) collective-permute-start(bf16[48,3072]{1,0:T(8,128)(2,1)S(1)} %get-tuple-element.235), channel_id=1, source_target_pairs={{0,8},{1,9},{2,10},{3,11},{4,12},{5,13},{6,14},{7,15},{8,0},{9,1},... | collective-permute-start | bytes 884744 | tf_op jit(solution)/shard_map/ppermute | solution.py:32
  237.0 23.5 %collective-permute-start.17 = (bf16[48,3072]{1,0:T(8,128)(2,1)S(1)}, bf16[48,3072]{1,0:T(8,128)(2,1)S(1)}, u32[]{:S(2)}, u32[]{:S(2)}) collective-permute-start(bf16[48,3072]{1,0:T(8,128)(2,1)S(1)} %get-tuple-element.237), channel_id=1, source_target_pairs={{0,16},{1,17},{2,18},{3,19},{4,20},{5,21},{6,22},{7,23},{8,24},{9,... | collective-permute-start | bytes 884744 | tf_op jit(solution)/shard_map/ppermute | solution.py:32
  240.0 20.5 %collective-permute-start.18 = (bf16[48,3072]{1,0:T(8,128)(2,1)S(1)}, bf16[48,3072]{1,0:T(8,128)(2,1)S(1)}, u32[]{:S(2)}, u32[]{:S(2)}) collective-permute-start(bf16[48,3072]{1,0:T(8,128)(2,1)S(1)} %get-tuple-element.236), channel_id=1, source_target_pairs={{0,24},{1,25},{2,26},{3,27},{4,28},{5,29},{6,30},{7,31},{8,16},{9,... | collective-permute-start | bytes 884744 | tf_op jit(solution)/shard_map/ppermute | solution.py:32
  242.8 47.2 %collective-permute-start.11 = (bf16[4,48,1536]{2,1,0:T(8,128)(2,1)}, bf16[4,48,1536]{2,1,0:T(8,128)(2,1)}, u32[]{:S(2)}, u32[]{:S(2)}) collective-permute-start(bf16[4,48,1536]{2,1,0:T(8,128)(2,1)} %slice.286), channel_id=1, source_target_pairs={{0,2},{1,5},{2,0},{3,7},{4,6},{5,1},{6,4},{7,3},{8,10},{9,13},{10,... | collective-permute-start | bytes 1769480 | tf_op jit(solution)/shard_map/ppermute | solution.py:32
  260.8 33.9 %collective-permute-start.25 = (bf16[48,3072]{1,0:T(8,128)(2,1)S(1)}, bf16[48,3072]{1,0:T(8,128)(2,1)}, u32[]{:S(2)}, u32[]{:S(2)}) collective-permute-start(bf16[48,3072]{1,0:T(8,128)(2,1)S(1)} %get-tuple-element.232), channel_id=1, source_target_pairs={{0,8},{1,9},{2,10},{3,11},{4,12},{5,13},{6,14},{7,15},{8,0},{9,1},... | collective-permute-start | bytes 884744 | tf_op jit(solution)/shard_map/ppermute | solution.py:32
  267.3 28.8 %collective-permute-start.26 = (bf16[48,3072]{1,0:T(8,128)(2,1)S(1)}, bf16[48,3072]{1,0:T(8,128)(2,1)}, u32[]{:S(2)}, u32[]{:S(2)}) collective-permute-start(bf16[48,3072]{1,0:T(8,128)(2,1)S(1)} %get-tuple-element.232), channel_id=1, source_target_pairs={{0,16},{1,17},{2,18},{3,19},{4,20},{5,21},{6,22},{7,23},{8,24},{9,... | collective-permute-start | bytes 884744 | tf_op jit(solution)/shard_map/ppermute | solution.py:32
  268.3 27.7 %collective-permute-start.27 = (bf16[48,3072]{1,0:T(8,128)(2,1)S(1)}, bf16[48,3072]{1,0:T(8,128)(2,1)}, u32[]{:S(2)}, u32[]{:S(2)}) collective-permute-start(bf16[48,3072]{1,0:T(8,128)(2,1)S(1)} %get-tuple-element.232), channel_id=1, source_target_pairs={{0,24},{1,25},{2,26},{3,27},{4,28},{5,29},{6,30},{7,31},{8,16},{9,... | collective-permute-start | bytes 884744 | tf_op jit(solution)/shard_map/ppermute | solution.py:32
  297.6 31.7 %collective-permute-start.28 = (bf16[4,48,1536]{2,1,0:T(8,128)(2,1)S(1)}, bf16[4,48,1536]{2,1,0:T(8,128)(2,1)S(1)}, u32[]{:S(2)}, u32[]{:S(2)}) collective-permute-start(bf16[4,48,1536]{2,1,0:T(8,128)(2,1)S(1)} %get-tuple-element.247), channel_id=1, source_target_pairs={{4,6},{5,7},{6,4},{7,5},{12,14},{13,15},{14,12},{15,13},{20,22},{2... | collective-permute-start | bytes 1769480 | tf_op jit(solution)/shard_map/ppermute | solution.py:32
  309.3 14.3 %collective-permute-start.20 = (bf16[48,1536]{1,0:T(8,128)(2,1)S(1)}, bf16[48,1536]{1,0:T(8,128)(2,1)S(1)}, u32[]{:S(2)}, u32[]{:S(2)}) collective-permute-start(bf16[48,1536]{1,0:T(8,128)(2,1)S(1)} %get-tuple-element.229), channel_id=1, source_target_pairs={{0,16},{1,17},{2,18},{3,19},{4,20},{5,21},{6,22},{7,23},{8,24},{9,... | collective-permute-start | bytes 442376 | tf_op jit(solution)/shard_map/ppermute | solution.py:32
  311.8 27.4 %collective-permute-start.29 = (bf16[4,48,1536]{2,1,0:T(8,128)(2,1)S(1)}, bf16[4,48,1536]{2,1,0:T(8,128)(2,1)S(1)}, u32[]{:S(2)}, u32[]{:S(2)}) collective-permute-start(bf16[4,48,1536]{2,1,0:T(8,128)(2,1)S(1)} %get-tuple-element.246), channel_id=1, source_target_pairs={{0,4},{1,5},{2,6},{3,7},{8,12},{9,13},{10,14},{11,15},{16,20},{17,... | collective-permute-start | bytes 1769480 | tf_op jit(solution)/shard_map/ppermute | solution.py:32
  314.5 24.7 %collective-permute-start.30 = (bf16[4,48,1536]{2,1,0:T(8,128)(2,1)S(1)}, bf16[4,48,1536]{2,1,0:T(8,128)(2,1)S(1)}, u32[]{:S(2)}, u32[]{:S(2)}) collective-permute-start(bf16[4,48,1536]{2,1,0:T(8,128)(2,1)S(1)} %get-tuple-element.245), channel_id=1, source_target_pairs={{0,6},{1,7},{2,4},{3,5},{8,14},{9,15},{10,12},{11,13},{16,22},{17,... | collective-permute-start | bytes 1769480 | tf_op jit(solution)/shard_map/ppermute | solution.py:32
  323.8 16.1 %collective-permute-start.22 = (bf16[4,48,1152]{2,1,0:T(8,128)(2,1)S(1)}, bf16[4,48,1152]{2,1,0:T(8,128)(2,1)S(1)}, u32[]{:S(2)}, u32[]{:S(2)}) collective-permute-start(bf16[4,48,1152]{2,1,0:T(8,128)(2,1)S(1)} %get-tuple-element.260), channel_id=1, source_target_pairs={{0,2},{1,3},{2,0},{3,1},{8,10},{9,11},{10,8},{11,9},{16,18},{17,19... | collective-permute-start | bytes 1327112 | tf_op jit(solution)/shard_map/ppermute | solution.py:32
  327.9 21.2 %collective-permute-start.23 = (bf16[4,48,1152]{2,1,0:T(8,128)(2,1)S(1)}, bf16[4,48,1152]{2,1,0:T(8,128)(2,1)S(1)}, u32[]{:S(2)}, u32[]{:S(2)}) collective-permute-start(bf16[4,48,1152]{2,1,0:T(8,128)(2,1)S(1)} %get-tuple-element.259), channel_id=1, source_target_pairs={{4,0},{5,1},{6,2},{7,3},{12,8},{13,9},{14,10},{15,11},{20,16},{21,... | collective-permute-start | bytes 1327112 | tf_op jit(solution)/shard_map/ppermute | solution.py:32
  329.2 19.9 %collective-permute-start.24 = (bf16[4,48,1152]{2,1,0:T(8,128)(2,1)S(1)}, bf16[4,48,1152]{2,1,0:T(8,128)(2,1)S(1)}, u32[]{:S(2)}, u32[]{:S(2)}) collective-permute-start(bf16[4,48,1152]{2,1,0:T(8,128)(2,1)S(1)} %get-tuple-element.258), channel_id=1, source_target_pairs={{4,2},{5,3},{6,0},{7,1},{12,10},{13,11},{14,8},{15,9},{20,18},{21,... | collective-permute-start | bytes 1327112 | tf_op jit(solution)/shard_map/ppermute | solution.py:32
  (77 other events, 1036.0 us)
Sparse Core Ops, SparseCore 0:
  11.4 87.7 all-gather.2
  290.1 65.6 all-gather.4
